TPU v7x, 128 devices: a whole 4x4x4 slice. The times are simulated.
128 devices in a mesh: batch: 4 (over x), span: 32 (over z, y, core).
Axes of the slice: x: 4, y: 4, z: 4, core: 2. Of those that a mesh axis runs over, the one named last changes fastest.
Arguments:
- heads_in: bfloat16 [131072, 1536], P(('batch', 'span')), parts along dimension 0, may hold values from -6 to 6
- writer: bfloat16 [131072, 64], P(('batch', 'span')), parts along dimension 0, may hold values from -6 to 6
- reader: bfloat16 [131072, 64], P(('batch', 'span')), parts along dimension 0, may hold values from -6 to 6
- log_decay: float32 [131072, 48], P(('batch', 'span')), parts along dimension 0, may hold values from -1 to 0
- norm_gain: float32 [1536], replicated, may hold values from 0.1 to 1.9
- merge_weight: bfloat16 [6144, 1536], replicated, may hold values from -0.078125 to 0.078125
- frame_owner: int32 [2048], P(('batch', 'span')), parts along dimension 0, may hold values from 0 to 31, as said below
Outputs:
- placed: bfloat16 [65536, 1536], P(('batch', 'span')), parts along dimension 0
There are 4 independent parts, one for each index of `batch`. A program takes and returns all parts, laid end to end along the dimension named above; an argument that names none is the same for every part. Nothing has to cross between parts.
Inputs may be any that keep to these rules, and one draw needn't show every extreme that they name: `frame_owner`: the 16 frames of one index of span go to 16 different owners. One owner receives at most 32 frames of a video, and some owner receives exactly 32.
All inputs are finite; a program needn't handle non-finite values.
Results may differ from a plain program's by a relative error of at most 0.0061.
Values may be sent and summed in bfloat16 or wider, within the bound.
A program may use at most 128 MiB of HBM per device.

v0:
```python
import jax
import jax.numpy as jnp
from jax import lax
from jax.sharding import PartitionSpec as P

FRAME_SIDE = 8


epsilon = 1e-05


def entering(part, axis, combine, identity):
    place = lax.axis_index(axis)
    gathered = jax.tree.map(lambda a: lax.all_gather(a, axis), part)
    state = jax.tree.map(lambda a, e: jnp.zeros_like(a) + jnp.asarray(e, a.dtype), part, identity)

    def one(turn, state):
        return combine(
            state, jax.tree.map(lambda a: lax.dynamic_index_in_dim(a, turn, 0, False), gathered)
        )

    return lax.fori_loop(0, place, one, state)


def block_summary(x_blk, write_blk, running, heads, head_dim):
    length, width = x_blk.shape
    to_end = jnp.exp(running[-1:, :] - running)
    scaled = (
        (x_blk.reshape(length, heads, head_dim) * to_end[:, :, None])
        .astype(jnp.bfloat16)
        .reshape(length, width)
    )
    block_state = lax.dot_general(
        write_blk, scaled, (((0,), (0,)), ((), ())), preferred_element_type=jnp.float32
    )
    return (block_state, jnp.exp(running[-1]))


def block_terms(x_blk, write_blk, read_blk, decay_blk, heads, head_dim):
    length, width = x_blk.shape
    running = jnp.cumsum(decay_blk, axis=0)
    running_heads = running.T
    scores = lax.dot_general(
        read_blk, write_blk, (((1,), (1,)), ((), ())), preferred_element_type=jnp.float32
    )
    row_index = lax.broadcasted_iota(jnp.int32, (length, length), 0)
    col_index = lax.broadcasted_iota(jnp.int32, (length, length), 1)
    causal = row_index >= col_index
    spacing = running_heads[:, :, None] - running_heads[:, None, :]
    spacing = jnp.where(causal[None], spacing, -jnp.inf)
    weights = (scores[None] * jnp.exp(spacing)).astype(jnp.bfloat16)
    values = x_blk.reshape(length, heads, head_dim)
    within = jnp.einsum(
        "hts,shp->thp", weights, values, preferred_element_type=jnp.float32
    ).reshape(length, width)
    block_state, block_decay = block_summary(x_blk, write_blk, running, heads, head_dim)
    return (within, block_state, block_decay, jnp.exp(running))


def carried(read_blk, carry_state, from_start, head_dim):
    rounded = carry_state.astype(jnp.bfloat16)
    projected = jnp.dot(read_blk, rounded, preferred_element_type=jnp.float32)
    return projected * jnp.repeat(from_start, head_dim, axis=1)


def advance(carry_state, block_decay, block_state, head_dim):
    return carry_state * jnp.repeat(block_decay, head_dim)[None, :] + block_state


def chain_states(own_decay, own_state, own_counts, head_dim):

    def chain_pair(earlier, latter):
        return (
            earlier[0] * latter[0],
            latter[1] + earlier[1] * jnp.repeat(latter[0], head_dim)[None, :],
            earlier[2] + latter[2],
        )

    identity = (jnp.ones_like(own_decay), jnp.zeros_like(own_state), jnp.zeros_like(own_counts))
    return entering((own_decay, own_state, own_counts), "span", chain_pair, identity)


def group_norm(mixed, norm_gain, head_dim):
    length, width = mixed.shape
    grouped = mixed.reshape(length, width // (2 * head_dim), 2 * head_dim)
    square_mean = jnp.mean(grouped * grouped, axis=-1, keepdims=True)
    scaled = (grouped * lax.rsqrt(square_mean + epsilon)).reshape(length, width)
    return (scaled * norm_gain[None, :]).astype(jnp.bfloat16)


def shuffle(normed, frame_side):
    width = normed.shape[1]
    half = frame_side // 2
    cells = normed.reshape(-1, half, 2, half, 2, width)
    cells = jnp.transpose(cells, (0, 1, 3, 2, 4, 5))
    return cells.reshape(-1, 4 * width)


def shards(heads_in, writer, reader, log_decay, norm_gain, merge_weight, frame_owner):
    tokens, width = heads_in.shape
    heads = log_decay.shape[1]
    head_dim = width // heads
    state_size = writer.shape[1]
    block_len = min(512, tokens)
    blocks = tokens // block_len
    span_count = lax.axis_size("span")
    frame_count = frame_owner.shape[0]
    capacity = min(2 * frame_count, span_count)
    frame_rows = FRAME_SIDE * FRAME_SIDE // 4
    input_blocks = heads_in.reshape(blocks, block_len, width)
    write_blocks = writer.reshape(blocks, block_len, state_size)
    read_blocks = reader.reshape(blocks, block_len, state_size)
    decay_blocks = log_decay.reshape(blocks, block_len, heads)
    owner_ids = lax.broadcasted_iota(jnp.int32, (frame_count, span_count), 1)
    owner_hits = (frame_owner[:, None] == owner_ids).astype(jnp.int32)
    own_counts = jnp.sum(owner_hits, axis=0).astype(jnp.float32)
    own_state = jnp.zeros((state_size, width), jnp.float32)
    own_decay = jnp.ones((heads,), jnp.float32)
    for block_index in range(blocks):
        running = jnp.cumsum(decay_blocks[block_index], axis=0)
        block_state, block_decay = block_summary(
            input_blocks[block_index], write_blocks[block_index], running, heads, head_dim
        )
        own_state = advance(own_state, block_decay, block_state, head_dim)
        own_decay = own_decay * block_decay
    _, incoming, before = chain_states(own_decay, own_state, own_counts, head_dim)

    def advance_block(carry_state, block_items):
        x_blk, write_blk, read_blk, decay_blk = block_items
        within, block_state, block_decay, from_start = block_terms(
            x_blk, write_blk, read_blk, decay_blk, heads, head_dim
        )
        output = within + carried(read_blk, carry_state, from_start, head_dim)
        return (advance(carry_state, block_decay, block_state, head_dim), output)

    _, mixed = lax.scan(
        advance_block, incoming, (input_blocks, write_blocks, read_blocks, decay_blocks)
    )
    mixed = mixed.reshape(tokens, width)
    normed = group_norm(mixed, norm_gain, head_dim)
    shuffled = shuffle(normed, FRAME_SIDE)
    earlier_counts = before.astype(jnp.int32)
    frame_rank = jnp.sum(owner_hits * earlier_counts[None, :], axis=1)
    slot_ids = jnp.full((span_count, 1), capacity, jnp.int32).at[frame_owner, 0].set(frame_rank)
    merged = jnp.dot(shuffled, merge_weight, preferred_element_type=jnp.float32).astype(
        jnp.bfloat16
    )
    merged = merged.reshape(frame_count, frame_rows, merged.shape[1])
    outgoing = (
        jnp.zeros((span_count, frame_rows, merged.shape[2]), jnp.bfloat16)
        .at[frame_owner]
        .set(merged)
    )
    arrived, places = (
        lax.all_to_all(outgoing, "span", split_axis=0, concat_axis=0, tiled=True),
        lax.all_to_all(slot_ids, "span", split_axis=0, concat_axis=0, tiled=True),
    )
    placed = (
        jnp.zeros((capacity, frame_rows, arrived.shape[2]), jnp.bfloat16)
        .at[places[:, 0]]
        .set(arrived, mode="drop")
    )
    return placed.reshape(capacity * frame_rows, arrived.shape[2])


def solution(mesh):
    return jax.shard_map(
        shards,
        mesh=mesh,
        in_specs=(
            P(("batch", "span"), None),
            P(("batch", "span"), None),
            P(("batch", "span"), None),
            P(("batch", "span"), None),
            P(),
            P(),
            P(("batch", "span")),
        ),
        out_specs=P(("batch", "span"), None),
        check_vma=False,
    )
```

profile of v0, /device:TPU:1, one launch (start us, length us, event | category | flops | bytes accessed | tf_op | source)
XLA Modules:
  0.0 377.5 jit_solution(617681871545023735)
XLA Ops:
  6.5 1.0 slice_bitcast_fusion.1
  7.5 1.2 reduce-window.24
  9.0 1.2 reduce-window.20
  11.0 3.2 fusion.33
  14.3 0.7 copy.104
  15.3 1.7 copy.105
  17.9 0.6 fusion.26
  18.5 1.4 fusion.27
  19.9 0.9 copy.95
  20.8 0.8 reshape.200
  21.6 0.6 dynamic-slice
  23.1 65.9 %all-reduce.1 = f32[1024]{0:T(1024)S(1)} all-reduce(f32[1024]{0:T(1024)S(1)} %convert_dynamic-update-slice_fusion), channel_id=3, replica_groups=mesh['batch'=4,'span'=32] {'span'}, use_global_device_ids=true, to_apply=%add.1 | all-reduce | flops 1024 | bytes 8192
  89.1 0.8 copy.96
  89.9 22.3 %all-gather.2 = f32[32,1,48]{2,1,0:T(1,128)S(1)} all-gather(f32[1,1,48]{2,1,0:T(1,128)S(1)} %bitcast.175), channel_id=1, replica_groups=mesh['batch'=4,'span'=32] {'span'}, dimensions={0}, use_global_device_ids=true | all-gather | bytes 6336 | tf_op jit(solution)/shard_map/all_gather | solution.py:14
  112.7 1.6 while.26
  112.9 1.2 bitcast_add_fusion.2
  114.8 79.8 %while.27 = (s32[]{:T(128)}, f32[64,1536]{1,0:T(8,128)S(1)}, f32[2,512,1536]{2,1,0:T(8,128)}, f32[2,512,48]{1,0,2:T(2,128)}, bf16[2,512,64]{2,1,0:T(8,128)(2,1)}...) while((s32[]{:T(128)}, f32[64,1536]{1,0:T(8,128)S(1)}, ...), condition=%wide.region_12.13_spmd, body=%wide.region_9.12_spmd.sunk | while | flops 1098203904 | bytes 53939716 | solution.py:136
  114.8 1.0 constant_dynamic-slice_fusion.7
  115.8 1.2 reduce-window.36
  117.2 0.8 copy_bitcast_fusion.11
  118.2 0.8 bitcast_exponential_fusion.2
  118.9 2.1 broadcast_in_dim.80
  121.0 2.4 copy.143
  123.4 2.3 fusion.61
  125.6 2.7 constant_dynamic-slice_fusion.6
  128.3 2.6 copy.141
  130.9 14.3 %fusion.62 = f32[48,32,512]{2,1,0:T(8,128)} fusion(bf16[512,48,32]{0,2,1:T(8,128)(2,1)} %bitcast.165, f32[48,512]{1,0:T(8,128)} %get-tuple-element.273, f32[512,512]{1,0:T(8,128)} %fusion.61, pred[512,512]{1,0:T(8,128)(4,1)S(1)} %iota_compare_fusion.3), kind=kOutput, calls=%fused_computation.10.clone.1 | convolution fusion | flops 855638016 | bytes 6127616 | tf_op jit(solution)/shard_map/while/body/eval_jaxpr/hts,shp->thp/dot_general | solution.py:53
  145.2 3.6 copy.142
  148.8 4.3 %fusion.63 = f32[2,512,1536]{2,1,0:T(8,128)} fusion(f32[2,512,1536]{2,1,0:T(8,128)} %get-tuple-element.316, s32[]{:T(128)} %get-tuple-element.314, f32[512,1536]{1,0:T(8,128)} %copy.142, f32[512,1536]{1,0:T(8,128)S(1)} %copy.143, f32[64,1536]{1,0:T(8,128)S(1)} %get-tuple-element.315, bf16[2,512,64]{2,1,0:T(8,128)(2,1)} %get-tuple-element.329), kind=kOutput, calls=%fused_computation.15.clone.1 | convolution fusion | flops 102334464 | bytes 9962496 | tf_op jit(solution)/shard_map/while/body/eval_jaxpr/dot_general | solution.py:62
  154.0 0.6 convolution_add_fusion.4
  154.7 1.0 constant_dynamic-slice_fusion.7
  155.7 1.2 reduce-window.36
  157.1 0.8 copy_bitcast_fusion.11
  158.1 0.8 bitcast_exponential_fusion.2
  158.8 2.1 broadcast_in_dim.80
  160.9 2.4 copy.143
  163.3 2.3 fusion.61
  165.5 2.7 constant_dynamic-slice_fusion.6
  168.2 2.6 copy.141
  170.9 14.3 %fusion.62 = f32[48,32,512]{2,1,0:T(8,128)} fusion(bf16[512,48,32]{0,2,1:T(8,128)(2,1)} %bitcast.165, f32[48,512]{1,0:T(8,128)} %get-tuple-element.273, f32[512,512]{1,0:T(8,128)} %fusion.61, pred[512,512]{1,0:T(8,128)(4,1)S(1)} %iota_compare_fusion.3), kind=kOutput, calls=%fused_computation.10.clone.1 | convolution fusion | flops 855638016 | bytes 6127616 | tf_op jit(solution)/shard_map/while/body/eval_jaxpr/hts,shp->thp/dot_general | solution.py:53
  185.1 3.6 copy.142
  188.7 4.3 %fusion.63 = f32[2,512,1536]{2,1,0:T(8,128)} fusion(f32[2,512,1536]{2,1,0:T(8,128)} %get-tuple-element.316, s32[]{:T(128)} %get-tuple-element.314, f32[512,1536]{1,0:T(8,128)} %copy.142, f32[512,1536]{1,0:T(8,128)S(1)} %copy.143, f32[64,1536]{1,0:T(8,128)S(1)} %get-tuple-element.315, bf16[2,512,64]{2,1,0:T(8,128)(2,1)} %get-tuple-element.329), kind=kOutput, calls=%fused_computation.15.clone.1 | convolution fusion | flops 102334464 | bytes 9962496 | tf_op jit(solution)/shard_map/while/body/eval_jaxpr/dot_general | solution.py:62
  193.9 0.6 convolution_add_fusion.4
  194.6 8.8 %mul.142 = f32[2,512,1536]{2,1,0:T(8,128)} multiply(f32[2,512,1536]{2,1,0:T(8,128)} %get-tuple-element.103, f32[2,512,1536]{2,1,0:T(8,128)} %get-tuple-element.103) | non-fusion elementwise | flops 1572864 | bytes 18874368 | tf_op jit(solution)/shard_map/mul | solution.py:86
  203.4 8.1 %reshape_reshape.3 = f32[16,4,2,4,2,1536]{5,4,3,2,1,0:T(2,128)} reshape(f32[2,512,1536]{2,1,0:T(8,128)} %get-tuple-element.103) | data formatting | bytes 12582912 | tf_op jit(solution)/shard_map/reshape;reshape | solution.py:85
  211.5 10.2 %copy.99 = f32[2,512,1536]{1,0,2:T(2,128)} copy(f32[2,512,1536]{2,1,0:T(8,128)} %mul.142) | data formatting | bytes 12582912 | tf_op jit(solution)/shard_map/mul | solution.py:86
  221.7 9.2 %mul.143 = f32[1024,24,64]{0,2,1:T(8,128)} reshape(f32[2,512,1536]{1,0,2:T(2,128)} %copy.99) | data formatting | bytes 12582912 | tf_op jit(solution)/shard_map/mul | solution.py:86
  231.0 3.7 reduce_sum.29
  234.9 7.1 %mul.144 = f32[1024,24,64]{2,1,0:T(8,128)} broadcast(f32[1024,24]{1,0:T(8,128)S(1)} %copy.100), dimensions={0,1} | broadcast | bytes 6389760 | tf_op jit(solution)/shard_map/mul | solution.py:87
  242.0 12.3 %mul.145 = f32[16,4,2,4,2,1536]{5,4,3,2,1,0:T(2,128)} reshape(f32[1024,24,64]{2,1,0:T(8,128)} %mul.144) | data formatting | bytes 12582912 | tf_op jit(solution)/shard_map/mul | solution.py:87
  254.3 10.5 %fusion.23 = bf16[16,4,4,2,2,1536]{5,4,2,3,1,0:T(2,128)(2,1)S(1)} fusion(f32[16,4,2,4,2,1536]{5,4,3,2,1,0:T(2,128)} %reshape_reshape.3, f32[16,4,2,4,2,1536]{5,4,3,2,1,0:T(2,128)} %mul.145, f32[1536]{0:T(1024)S(1)} %copy-done.9), kind=kLoop, calls=%fused_computation.45 | loop fusion | flops 4718592 | bytes 15734784 | tf_op jit(solution)/shard_map/transpose | solution.py:95
  264.8 4.9 %copy.101 = bf16[16,4,4,2,2,1536]{5,4,3,2,1,0:T(2,128)(2,1)} copy(bf16[16,4,4,2,2,1536]{5,4,2,3,1,0:T(2,128)(2,1)S(1)} %fusion.23) | data formatting | bytes 6291456 | tf_op jit(solution)/shard_map/transpose | solution.py:95
  269.7 7.0 %reshape.204 = bf16[256,6144]{1,0:T(8,128)(2,1)S(1)} reshape(bf16[16,4,4,2,2,1536]{5,4,3,2,1,0:T(2,128)(2,1)} %copy.101) | data formatting | bytes 6291456 | tf_op jit(solution)/shard_map/reshape | solution.py:96
  276.9 0.6 scatter_custom_fusion
  277.5 0.7 copy.94
  278.2 45.4 %all-to-all-start = ((s32[32,1,1]{2,1,0:T(1,128)}), s32[32,1,1]{2,1,0:T(1,128)S(1)}, u32[]{:S(2)}, u32[]{:S(2)}) async-start(s32[32,1,1]{2,1,0:T(1,128)} %copy.94), calls=%async_computation | async-start | bytes 32768 | tf_op jit(solution)/shard_map/all_to_all | solution.py:156
  323.6 9.9 %convolution_convert_fusion = bf16[256,1536]{1,0:T(8,128)(2,1)} fusion(bf16[256,6144]{1,0:T(8,128)(2,1)S(1)} %reshape.204, bf16[6144,1536]{1,0:T(8,128)(2,1)} %param.16), kind=kOutput, calls=%fused_computation.50 | convolution fusion | flops 4832231424 | bytes 22806528 | tf_op jit(solution)/shard_map/dot_general | solution.py:145
  333.5 1.3 broadcast.85.clone
  334.9 3.1 scatter_fusion
  338.0 7.4 %all-to-all-start.1 = ((bf16[32,16,1536]{2,1,0:T(8,128)(2,1)}), bf16[32,16,1536]{2,1,0:T(8,128)(2,1)S(1)}, u32[]{:S(2)}, u32[]{:S(2)}) async-start(bf16[32,16,1536]{2,1,0:T(8,128)(2,1)} %scatter_fusion), calls=%async_computation.1 | async-start | bytes 3145728 | tf_op jit(solution)/shard_map/all_to_all | solution.py:155
  345.4 0.7 reduce.7
  346.0 21.5 %all-to-all-done.1 = bf16[32,16,1536]{2,1,0:T(8,128)(2,1)S(1)} async-done(((bf16[32,16,1536]{2,1,0:T(8,128)(2,1)}), bf16[32,16,1536]{2,1,0:T(8,128)(2,1)S(1)}, u32[]{:S(2)}, u32[]{:S(2)}) %all-to-all-start.1) | async-done | bytes 1572896 | tf_op jit(solution)/shard_map/all_to_all | solution.py:155
  367.7 1.8 scatter_fusion.1
  369.5 1.1 copy-done.3
  (95 shorter events, 7.2 us)
Async XLA Ops:
  6.5 106.1 %all-gather.5.cloned.1.call-start = ((), (), s32[]{:S(2)}) async-start(), calls=%async_computation.2 | async-start | bytes 12976128 | tf_op jit(solution)/shard_map/all_gather | solution.py:14
  17.0 0.9 copy-start.5
  17.9 2.9 copy-start.4
  17.9 3.7 copy-start.13
  17.9 5.0 %copy-start.11 = (s32[16]{0:T(128)S(1)}, s32[16]{0:T(128)}, u32[]{:S(2)}) copy-start(s32[16]{0:T(128)} %param.17) | copy-start | bytes 196
  17.9 71.1 %copy-start.6 = (bf16[1024,64]{0,1:T(8,128)(2,1)S(1)}, bf16[1024,64]{0,1:T(8,128)(2,1)}, u32[]{:S(2)}) copy-start(bf16[1024,64]{0,1:T(8,128)(2,1)} %param.13) | copy-start | bytes 393220
  114.3 0.5 copy-start.7
  148.8 4.3 %copy-start = (bf16[1,512,1536]{1,2,0:T(8,128)(2,1)S(1)}, bf16[1,512,1536]{1,2,0:T(8,128)(2,1)}, u32[]{:S(2)}) copy-start(bf16[1,512,1536]{1,2,0:T(8,128)(2,1)} %copy.141) | copy-start | bytes 4718596 | tf_op jit(solution)/shard_map/while
  148.8 4.3 %copy-start.1 = (f32[512,48]{0,1:T(8,128)S(1)}, f32[512,48]{0,1:T(8,128)}, u32[]{:S(2)}) copy-start(f32[512,48]{0,1:T(8,128)} %get-tuple-element.272) | copy-start | bytes 294916 | tf_op jit(solution)/shard_map/while
  153.1 0.9 copy-start.2
  188.7 4.3 %copy-start = (bf16[1,512,1536]{1,2,0:T(8,128)(2,1)S(1)}, bf16[1,512,1536]{1,2,0:T(8,128)(2,1)}, u32[]{:S(2)}) copy-start(bf16[1,512,1536]{1,2,0:T(8,128)(2,1)} %copy.141) | copy-start | bytes 4718596 | tf_op jit(solution)/shard_map/while
  188.7 4.3 %copy-start.1 = (f32[512,48]{0,1:T(8,128)S(1)}, f32[512,48]{0,1:T(8,128)}, u32[]{:S(2)}) copy-start(f32[512,48]{0,1:T(8,128)} %get-tuple-element.272) | copy-start | bytes 294916 | tf_op jit(solution)/shard_map/while
  193.0 0.9 copy-start.2
  242.0 12.3 %copy-start.9 = (f32[1536]{0:T(1024)S(1)}, f32[1536]{0:T(1024)}, u32[]{:S(2)}) copy-start(f32[1536]{0:T(1024)} %param.15) | copy-start | bytes 18436
  269.7 7.0 %copy-start.8 = (f32[32]{0:T(128)S(1)}, f32[32]{0:T(128)}, u32[]{:S(2)}) copy-start(f32[32]{0:T(128)} %copy-done.7) | copy-start | bytes 388
  269.7 7.0 %copy-start.12 = (s32[16]{0:T(128)S(1)}, s32[16]{0:T(128)}, u32[]{:S(2)}) copy-start(s32[16]{0:T(128)} %param.17) | copy-start | bytes 196
  269.7 7.2 %copy-start.10 = (s32[16]{0:T(128)S(1)}, s32[16]{0:T(128)}, u32[]{:S(2)}) copy-start(s32[16]{0:T(128)} %compare_select_fusion.1) | copy-start | bytes 196
  278.2 59.8 %all-to-all-start = ((s32[32,1,1]{2,1,0:T(1,128)}), s32[32,1,1]{2,1,0:T(1,128)S(1)}, u32[]{:S(2)}, u32[]{:S(2)}) async-start(s32[32,1,1]{2,1,0:T(1,128)} %copy.94), calls=%async_computation | async-start | bytes 32768 | tf_op jit(solution)/shard_map/all_to_all | solution.py:156
  338.0 29.6 %all-to-all-start.1 = ((bf16[32,16,1536]{2,1,0:T(8,128)(2,1)}), bf16[32,16,1536]{2,1,0:T(8,128)(2,1)S(1)}, u32[]{:S(2)}, u32[]{:S(2)}) async-start(bf16[32,16,1536]{2,1,0:T(8,128)(2,1)} %scatter_fusion), calls=%async_computation.1 | async-start | bytes 3145728 | tf_op jit(solution)/shard_map/all_to_all | solution.py:155
  369.5 1.1 copy-start.3
Sparse Core Ops, SparseCore 0:
  20.0 66.8 all-gather.4
where the time goes:
time: 381 us; the launch traced here: 377 us
  local copies, waits for them, and re-layouts  110 us (29%)
  blocking collectives  88.1 us (23%)
  matrix products  54.8 us (14%)
  starting transfers between devices  52.8 us (14%)
  other arithmetic  36 us (9%)
  waiting for transfers between devices  21.5 us (6%)
  between operations  14.3 us (4%)
    unnamed x1, blocking collectives  65.9 us
    all_to_all x1, starting transfers between devices, shards(): lax.all_to_all(slot_ids, 'span', split_axis=0, concat_axis=0, tiled=True)  45.4 us
    dot_general x2, matrix products, block_terms(): jnp.einsum('hts,shp->thp', weights, values, preferred_element_type=jnp.fl...  28.6 us
    all_gather x1, blocking collectives, entering(): gathered = jax.tree.map(lambda a: lax.all_gather(a, axis), part)  22.3 us
    all_to_all x1, waiting for transfers between devices, shards(): lax.all_to_all(outgoing, 'span', split_axis=0, concat_axis=0, tiled=True)  21.5 us
    mul x2, local copies, waits for them, and re-layouts, group_norm(): square_mean = jnp.mean(grouped * grouped, axis=-1, keepdims=True)  19.5 us
    mul x2, local copies, waits for them, and re-layouts, group_norm(): scaled = (grouped * lax.rsqrt(square_mean + epsilon)).reshape(length, width)  19.4 us
    dynamic_slice x6, local copies, waits for them, and re-layouts, shards(): lax.scan(advance_block, incoming, (input_blocks, write_blocks, read_block...  12.5 us
  transfers between devices with their start and end apart: 3, of which 1 were waited for; matrix products, arithmetic and copies ran while one was open for 5% of the time, Pallas kernels for 0%

commit v1 on v0

v1 whole, which is shorter than its diff:
```python
import functools

import jax
import jax.numpy as jnp
from jax import lax
from jax.experimental import pallas as pl
from jax.experimental.pallas import tpu as pltpu
from jax.sharding import PartitionSpec as P

MESH = pl.DeviceIdType.MESH
F32 = jnp.float32
BF16 = jnp.bfloat16
EPSILON = 1e-05
FRAME_SIDE = 8
CHUNK = 128
LANES = 256
GROUP = 64


def dot(a, b):
    return lax.dot_general(a, b, (((1,), (0,)), ((), ())), preferred_element_type=F32)


def iota(shape, axis):
    return lax.broadcasted_iota(jnp.int32, shape, axis)


def ones_where(condition):
    return jnp.where(condition, 1.0, 0.0).astype(BF16)


def token_of_row(row):
    q, rest = row >> 5, row & 31
    frame, i2, j2 = rest >> 4, (rest >> 2) & 3, rest & 3
    return frame * 64 + (2 * i2 + (q >> 1)) * 8 + 2 * j2 + (q & 1)


def two_parts(values):
    high = values.astype(BF16)
    low = (values - high.astype(F32)).astype(BF16)
    return jnp.where(iota(values.shape, 1) < 64, high.astype(F32), low.astype(F32)).astype(BF16)


def kernel(
    n, x_h, w_h, r_h, d_h, g_h, o_h, wm_h, out_h,
    x_v, w_v, r_v, d_v, g_v, o_v, wm_v,
    cum_l, expand, block_diag, perm, xs_v, out_arg, dev_arg, state, rp_v, ml_v, od_v, a_v,
    meta_s, meta_r, send1, recv1, decays, send2, recv2, enter, sel_s, sel_r, send3, recv3, out_v,
    x_sem, in_sem, wm_sem, out_sem, meta_sem, one_sem, two_sem, del_s_sem, del_r_sem,
):
    me = lax.axis_index("span")
    chunks, _, width = x_v.shape
    heads = d_h.shape[1]
    tiles = width // LANES
    frames = o_h.shape[1]
    rows = 16

    small = [
        pltpu.make_async_copy(s, d, in_sem.at[k])
        for k, (s, d) in enumerate(((d_h, d_v), (w_h, w_v), (r_h, r_v), (g_h, g_v), (o_h, o_v)))
    ]
    loads = [pltpu.make_async_copy(x_h.at[c], x_v.at[c], x_sem.at[c]) for c in range(chunks)]
    weights = [
        pltpu.make_async_copy(wm_h.at[:, pl.ds(t * LANES, LANES)], wm_v.at[t], wm_sem.at[t])
        for t in range(tiles)
    ]
    for copy in small + loads + weights:
        copy.start()

    barrier = pltpu.get_barrier_semaphore()

    def greet(k, _):
        pl.semaphore_signal(
            barrier, inc=1, device_id={"span": lax.rem(me + k, n)}, device_id_type=MESH
        )
        return 0

    lax.fori_loop(1, n, greet, 0)

    row_l, col_l = iota((CHUNK, CHUNK), 0), iota((CHUNK, CHUNK), 1)
    token = token_of_row(row_l)
    lower = ones_where(col_l <= row_l)
    lower_p = ones_where(col_l <= token)
    perm[...] = ones_where(col_l == token)
    for k in range(3):
        cum_l[0:CHUNK, k * CHUNK : (k + 1) * CHUNK] = lower
        cum_l[CHUNK : 2 * CHUNK, k * CHUNK : (k + 1) * CHUNK] = lower_p
    head_dim_shift = (width // heads).bit_length() - 1
    expand[...] = ones_where(
        (iota((128, width), 0) & 63) == (iota((128, width), 1) >> head_dim_shift)
    )
    block_diag[...] = ones_where(
        (iota((LANES, LANES), 0) >> 6) == (iota((LANES, LANES), 1) >> 6)
    )
    state[...] = jnp.zeros_like(state)
    meta_s[...] = jnp.full(meta_s.shape, -1.0, F32)
    for copy in small:
        copy.wait()

    owners = o_v[...].astype(F32)
    meta_s[1:2, 0:frames] = owners
    owner_rows = jnp.broadcast_to(owners, (8, frames)).astype(BF16)
    spread = ones_where(
        iota((frames, frames * rows), 0) == (iota((frames, frames * rows), 1) >> 4)
    )
    owner_row = dot(owner_rows, spread)[0:1]
    shape = (n * rows, frames * rows)
    sel_s[...] = ones_where(
        ((iota(shape, 0) >> 4).astype(F32) == owner_row)
        & ((iota(shape, 0) & 15) == (iota(shape, 1) & 15))
    )

    def summarize(c, before):
        start = pl.multiple_of(c * CHUNK, CHUNK)
        decay = d_v[pl.ds(start, CHUNK), :]
        gap = jnp.zeros((CHUNK, 64 - heads), F32)
        decay = jnp.concatenate([decay, gap, decay, gap], axis=1)
        high = decay.astype(BF16)
        left = decay - high.astype(F32)
        middle = left.astype(BF16)
        low = (left - middle.astype(F32)).astype(BF16)
        both = dot(cum_l[...], jnp.concatenate([high, middle, low], axis=0))
        running, running_p = both[0:CHUNK], both[CHUNK : 2 * CHUNK]
        ref = running[CHUNK // 2 - 1 : CHUNK // 2]
        total = running[CHUNK - 1 : CHUNK]
        out_arg[c] = running_p - ref
        dev_arg[c] = running_p + before
        row = iota((16, 128), 0)
        extra = jnp.where(row == 0, ref, jnp.where(row == 1, total, total - ref))
        factors = two_parts(jnp.exp(jnp.concatenate([ref - running, extra], axis=0)))
        writes = w_v[pl.ds(start, CHUNK), :]
        pltpu.make_async_copy(x_h.at[c], x_v.at[c], x_sem.at[c]).wait()
        for t in range(tiles):
            cols = slice(t * LANES, (t + 1) * LANES)
            full = dot(factors, expand[:, cols])
            scaled = (x_v[c, :, cols].astype(F32) * full[0:CHUNK]).astype(BF16)
            own = lax.dot_general(
                writes, scaled, (((0,), (0,)), ((), ())), preferred_element_type=F32
            )
            earlier = state[:, cols]
            xs_v[c, t, 0:CHUNK] = scaled
            xs_v[c, t, CHUNK : CHUNK + 64] = (earlier * full[CHUNK : CHUNK + 1]).astype(BF16)
            state[:, cols] = (
                earlier * full[CHUNK + 1 : CHUNK + 2] + own * full[CHUNK + 2 : CHUNK + 3]
            )
        return before + total

    total = lax.fori_loop(0, chunks, summarize, jnp.zeros((1, 128), F32))
    meta_s[0:1, :] = total
    for a in range(8):
        for b in range(4):
            send1[a * 4 + b] = state[8 * a : 8 * a + 8, 384 * b : 384 * b + 384].astype(BF16)

    pl.semaphore_wait(barrier, n - 1)

    def remote(source, target, sems, d):
        return pltpu.make_async_remote_copy(
            src_ref=source,
            dst_ref=target,
            send_sem=sems.at[0],
            recv_sem=sems.at[1],
            device_id={"span": d},
            device_id_type=MESH,
        )

    def all_of(ref, sem):
        part = ref.at[pl.ds(0, n - 1)]
        pltpu.make_async_copy(part, part, sem).wait()

    def send_meta(k, _):
        remote(meta_s, meta_r.at[me], meta_sem, lax.rem(me + k, n)).start()
        return 0

    lax.fori_loop(1, n, send_meta, 0)

    def send_one(k, _):
        d = lax.rem(me + k, n)
        remote(send1.at[d], recv1.at[me], one_sem, d).start()
        return 0

    lax.fori_loop(1, n, send_one, 0)
    meta_r[me] = meta_s[...]
    recv1[me] = send1[me]

    causal = iota((CHUNK, CHUNK), 1) <= token_of_row(iota((CHUNK, CHUNK), 0))

    def local(c, _):
        start = pl.multiple_of(c * CHUNK, CHUNK)
        reads = dot(perm[...], r_v[pl.ds(start, CHUNK), :]).astype(BF16)
        rp_v[pl.ds(start, CHUNK), :] = reads
        scores = lax.dot_general(
            reads, w_v[pl.ds(start, CHUNK), :], (((1,), (1,)), ((), ())),
            preferred_element_type=F32,
        )
        masked = jnp.where(causal, scores, 0.0).astype(BF16)
        left = jnp.concatenate([masked, reads], axis=1)
        factors = two_parts(jnp.exp(jnp.concatenate([out_arg[c], dev_arg[c]], axis=0)))
        for t in range(tiles):
            full = dot(factors, expand[:, t * LANES : (t + 1) * LANES])
            mixed = dot(left, xs_v[c, t])
            ml_v[t, pl.ds(start, CHUNK), :] = mixed * full[0:CHUNK]
            od_v[t, pl.ds(start, CHUNK), :] = full[CHUNK : 2 * CHUNK]
        return 0

    lax.fori_loop(0, chunks, local, 0)

    all_of(meta_r, meta_sem.at[1])
    totals = meta_r[:, 0, :]
    factors = two_parts(jnp.exp(totals))
    for b in range(4):
        decays[b] = dot(factors, expand[:, 384 * b : 384 * b + 384])
    owned = jnp.max(jnp.where(meta_r[:, 1, :] == me.astype(F32), 1.0, 0.0), axis=1, keepdims=True)
    owned = jnp.broadcast_to(owned, (n, 128))
    rank = dot(ones_where(iota((n, n), 1) < iota((n, n), 0)), owned.astype(BF16))
    place = jnp.where(owned > 0.0, rank + 1.0, 0.0)[:, 0:1]
    shape = (n, n * rows)
    place_row = jnp.sum(
        jnp.where((iota(shape, 1) >> 4) == iota(shape, 0), place, 0.0), axis=0, keepdims=True
    )
    shape = (n * rows, n * rows)
    sel_r[...] = ones_where(
        (((iota(shape, 0) >> 4) + 1).astype(F32) == place_row)
        & ((iota(shape, 0) & 15) == (iota(shape, 1) & 15))
    )

    all_of(recv1, one_sem.at[1])
    quarter = lax.rem(me, 4)
    carry = jnp.zeros(recv1.shape[1:], F32)
    for i in range(n):
        send2[i] = carry.astype(BF16)
        if i < n - 1:
            carry = carry * decays[quarter, i : i + 1, :] + recv1[i].astype(F32)

    def send_two(k, _):
        d = lax.rem(me + k, n)
        remote(send2.at[d], recv2.at[me], two_sem, d).start()
        return 0

    lax.fori_loop(1, n, send_two, 0)
    recv2[me] = send2[me]
    all_of(recv2, two_sem.at[1])
    for a in range(8):
        for b in range(4):
            enter[8 * a : 8 * a + 8, 384 * b : 384 * b + 384] = recv2[a * 4 + b].astype(F32)

    def norm(t, _):
        first = pl.multiple_of(t * LANES, LANES)
        entering = enter[:, pl.ds(first, LANES)].astype(BF16)
        gain = g_v[:, pl.ds(first, LANES)]
        for b in range(chunks // 2):
            part = slice(2 * b * CHUNK, 2 * (b + 1) * CHUNK)
            mixed = ml_v[t, part] + od_v[t, part] * dot(rp_v[part], entering)
            squares = dot((mixed * mixed).astype(BF16), block_diag[...])
            normed = mixed * lax.rsqrt(squares * (1.0 / GROUP) + EPSILON) * gain
            normed = normed.astype(BF16)
            for c in range(2):
                for q in range(4):
                    a_v[
                        (2 * b + c) * 32 : (2 * b + c + 1) * 32,
                        pl.ds(pl.multiple_of(q * width + t * LANES, LANES), LANES),
                    ] = normed[c * CHUNK + q * 32 : c * CHUNK + (q + 1) * 32]
        return 0

    lax.fori_loop(0, tiles, norm, 0)

    def deliver(t, _):
        pltpu.make_async_copy(
            wm_h.at[:, pl.ds(pl.multiple_of(t * LANES, LANES), LANES)], wm_v.at[t], wm_sem.at[t]
        ).wait()
        merged = dot(a_v[...], wm_v[t]).astype(BF16)
        send3[t] = dot(sel_s[...], merged).astype(BF16).reshape(n, rows, LANES)

        def send(k, _):
            d = lax.rem(me + k, n)
            pltpu.make_async_remote_copy(
                src_ref=send3.at[t, d],
                dst_ref=recv3.at[t, me],
                send_sem=del_s_sem,
                recv_sem=del_r_sem.at[t],
                device_id={"span": d},
                device_id_type=MESH,
            ).start()
            return 0

        lax.fori_loop(1, n, send, 0)
        recv3[t, me] = send3[t, me]
        return 0

    lax.fori_loop(0, tiles, deliver, 0)

    def put(t):
        return pltpu.make_async_copy(
            out_v.at[t], out_h.at[:, pl.ds(pl.multiple_of(t * LANES, LANES), LANES)], out_sem
        )

    def arrive(t, _):
        part = recv3.at[t, pl.ds(0, n - 1)]
        pltpu.make_async_copy(part, part, del_r_sem.at[t]).wait()
        out_v[t] = dot(sel_r[...], recv3[t].reshape(n * rows, LANES)).astype(BF16)
        put(t).start()
        return 0

    lax.fori_loop(0, tiles, arrive, 0)
    pltpu.make_async_copy(out_v, out_v, out_sem).wait()
    one_meta = meta_r.at[pl.ds(0, n - 1)]
    pltpu.make_async_copy(one_meta, one_meta, meta_sem.at[0]).wait()
    all_of(send1, one_sem.at[0])
    all_of(send2, two_sem.at[0])

    def sent(t, _):
        part = send3.at[t, pl.ds(0, n - 1)]
        pltpu.make_async_copy(part, part, del_s_sem).wait()
        return 0

    lax.fori_loop(0, tiles, sent, 0)


def shards(heads_in, writer, reader, log_decay, norm_gain, merge_weight, frame_owner):
    tokens, width = heads_in.shape
    n = lax.axis_size("span")
    chunks = tokens // CHUNK
    tiles = width // LANES
    frames = frame_owner.shape[0]
    state_size = writer.shape[1]
    deep, out_width = merge_weight.shape
    assert (n, state_size, width, out_width, frames) == (32, 64, 1536, 1536, 16)
    vmem, dma = pltpu.VMEM, pltpu.SemaphoreType.DMA
    anywhere = pl.BlockSpec(memory_space=pl.ANY)
    return pl.pallas_call(
        functools.partial(kernel, n),
        out_shape=jax.ShapeDtypeStruct((n * 16, out_width), BF16),
        in_specs=[anywhere] * 7,
        out_specs=anywhere,
        scratch_shapes=[
            vmem((chunks, CHUNK, width), BF16),
            vmem(writer.shape, BF16),
            vmem(reader.shape, BF16),
            vmem(log_decay.shape, F32),
            vmem((1, width), F32),
            vmem((1, frames), jnp.int32),
            vmem((tiles, deep, LANES), BF16),
            vmem((2 * CHUNK, 3 * CHUNK), BF16),
            vmem((128, width), BF16),
            vmem((LANES, LANES), BF16),
            vmem((CHUNK, CHUNK), BF16),
            vmem((chunks, tiles, CHUNK + state_size, LANES), BF16),
            vmem((chunks, CHUNK, 128), F32),
            vmem((chunks, CHUNK, 128), F32),
            vmem((state_size, width), F32),
            vmem((tokens, state_size), BF16),
            vmem((tiles, tokens, LANES), F32),
            vmem((tiles, tokens, LANES), F32),
            vmem((tokens // 4, deep), BF16),
            vmem((8, 128), F32),
            vmem((n, 8, 128), F32),
            vmem((n, 8, 384), BF16),
            vmem((n, 8, 384), BF16),
            vmem((4, n, 384), F32),
            vmem((n, 8, 384), BF16),
            vmem((n, 8, 384), BF16),
            vmem((state_size, width), F32),
            vmem((n * 16, frames * 16), BF16),
            vmem((n * 16, n * 16), BF16),
            vmem((tiles, n, 16, LANES), BF16),
            vmem((tiles, n, 16, LANES), BF16),
            vmem((tiles, n * 16, LANES), BF16),
            dma((chunks,)),
            dma((5,)),
            dma((tiles,)),
            dma,
            dma((2,)),
            dma((2,)),
            dma((2,)),
            dma,
            dma((tiles,)),
        ],
        compiler_params=pltpu.CompilerParams(
            collective_id=0, has_side_effects=True, vmem_limit_bytes=62 * 1024 * 1024
        ),
    )(
        heads_in.reshape(chunks, CHUNK, width),
        writer,
        reader,
        log_decay,
        norm_gain.reshape(1, width),
        frame_owner.reshape(1, frames),
        merge_weight,
    )


def solution(mesh):
    return jax.shard_map(
        shards,
        mesh=mesh,
        in_specs=(
            P(("batch", "span"), None),
            P(("batch", "span"), None),
            P(("batch", "span"), None),
            P(("batch", "span"), None),
            P(),
            P(),
            P(("batch", "span")),
        ),
        out_specs=P(("batch", "span"), None),
        check_vma=False,
    )
```

time: 381 us -> 70 us (0.18)
  local copies, waits for them, and re-layouts: 110 us -> 9.37 us
  blocking collectives: 88.1 us -> 0 us
  Pallas kernels: 0 us -> 60.4 us
  matrix products: 54.8 us -> 0 us
  starting transfers between devices: 52.8 us -> 0 us
  other arithmetic: 36 us -> 0 us
  waiting for transfers between devices: 21.5 us -> 0 us
  between operations: 14.3 us -> 0.01 us
    unnamed x1 -> x0, blocking collectives: 65.9 us -> none
    pallas_call x0 -> x1, Pallas kernels: none -> 60.4 us  [shards(): pl.pallas_call(functools.partial(kernel, n), out_shape=jax.ShapeDtypeStru...]
    dot_general x11 -> x0, matrix products: 54.8 us -> none  [the longest x2 28.6 us: block_terms(): jnp.einsum('hts,shp->thp', weights, values, preferred_element_type=jnp.fl...]
    all_to_all x2 -> x0, starting transfers between devices: 52.8 us -> none  [the longest x1 45.4 us: shards(): lax.all_to_all(slot_ids, 'span', split_axis=0, concat_axis=0, tiled=True)]
    mul x8 -> x0, local copies, waits for them, and re-layouts: 39.2 us -> none  [the longest x2 19.5 us: group_norm(): square_mean = jnp.mean(grouped * grouped, axis=-1, keepdims=True)]
    all_gather x1 -> x0, blocking collectives: 22.3 us -> none  [entering(): gathered = jax.tree.map(lambda a: lax.all_gather(a, axis), part)]
    all_to_all x2 -> x0, waiting for transfers between devices: 21.5 us -> none  [the longest x1 21.5 us: shards(): lax.all_to_all(outgoing, 'span', split_axis=0, concat_axis=0, tiled=True)]
    reshape x6 -> x1, local copies, waits for them, and re-layouts: 19.7 us -> 1.3 us  [shards(): norm_gain.reshape(1, width)]
  transfers between devices with their start and end apart: 3 -> 0, of which waited for: 1 -> 0; matrix products, arithmetic and copies ran while one was open for 5% -> 0% of each run, Pallas kernels for 0% -> 0%
where the time goes in v1:
time: 70 us; the launch traced here: 69.8 us
  Pallas kernels  60.4 us (86%)
  local copies, waits for them, and re-layouts  9.37 us (13%)
    pallas_call x1, Pallas kernels, shards(): pl.pallas_call(functools.partial(kernel, n), out_shape=jax.ShapeDtypeStru...  60.4 us
    unnamed x4, local copies, waits for them, and re-layouts  8.07 us

profile of v1, /device:TPU:1, one launch (start us, length us, event | category | flops | bytes accessed | tf_op | source)
XLA Modules:
  0.0 69.8 jit_solution(3342655128199703379)
XLA Ops:
  0.0 1.3 %reshape.10.g_h = f32[1,1536]{1,0:T(1,128)} reshape(f32[1536]{0:T(1024)} %param.11) | data formatting | bytes 12288 | tf_op jit(solution)/shard_map/reshape | solution.py:385
  1.3 1.7 %copy.8.w_h = bf16[1024,64]{1,0:T(8,128)(2,1)} copy(bf16[1024,64]{0,1:T(8,128)(2,1)} %param.8) | data formatting | bytes 262144 | tf_op args[1]
  3.0 1.8 %copy.9.r_h = bf16[1024,64]{1,0:T(8,128)(2,1)} copy(bf16[1024,64]{0,1:T(8,128)(2,1)} %param.9) | data formatting | bytes 262144 | tf_op args[2]
  4.8 1.9 %copy.10.d_h = f32[1024,48]{1,0:T(8,128)} copy(f32[1024,48]{0,1:T(8,128)} %param.10) | data formatting | bytes 393216 | tf_op args[3]
  6.7 60.4 %shard_map.73 = bf16[512,1536]{1,0:T(8,128)(2,1)} custom-call(bf16[8,128,1536]{2,1,0:T(8,128)(2,1)} %bitcast.2, bf16[1024,64]{1,0:T(8,128)(2,1)} %copy.8.w_h, bf16[1024,64]{1,0:T(8,128)(2,1)} %copy.9.r_h, f32[1024,48]{1,0:T(8,128)} %copy.10.d_h, f32[1,1536]{1,0:T(1,128)} %reshape.10.g_h, s32[1,16]{1,0:T(1,128)} %bitcast.3, bf16[6144,1536]{1,0:T(8,128)(2,1)} %wm_h.1), custom_call_target="tpu_custom_call" | custom-call | tf_op jit(solution)/shard_map/pallas_call | solution.py:329
  67.1 2.7 %copy.12 = bf16[512,1536]{1,0:T(8,128)(2,1)} copy(bf16[512,1536]{1,0:T(8,128)(2,1)} %shard_map.73) | data formatting | bytes 3145728

commit v2 on v1

--- a/solution.py
+++ b/solution.py
@@ -21,6 +21,10 @@
     return lax.dot_general(a, b, (((1,), (0,)), ((), ())), preferred_element_type=F32)
 
 
+def dot_t(a, b):
+    return lax.dot_general(a, b, (((1,), (1,)), ((), ())), preferred_element_type=F32)
+
+
 def iota(shape, axis):
     return lax.broadcasted_iota(jnp.int32, shape, axis)
 
@@ -45,12 +49,12 @@
     n, x_h, w_h, r_h, d_h, g_h, o_h, wm_h, out_h,
     x_v, w_v, r_v, d_v, g_v, o_v, wm_v,
     cum_l, expand, block_diag, perm, xs_v, out_arg, dev_arg, state, rp_v, ml_v, od_v, a_v,
-    meta_s, meta_r, send1, recv1, decays, send2, recv2, enter, sel_s, sel_r, send3, recv3, out_v,
-    x_sem, in_sem, wm_sem, out_sem, meta_sem, one_sem, two_sem, del_s_sem, del_r_sem,
+    meta_s, meta_r, send1, recv1, decays, send2, recv2, enter, sel_s, sel_r, send3, recv3,
+    x_sem, in_sem, wm_sem, meta_sem, one_sem, two_sem, del_s_sem, del_r_sem,
 ):
     me = lax.axis_index("span")
     chunks, _, width = x_v.shape
-    heads = d_h.shape[1]
+    heads = d_h.shape[0]
     tiles = width // LANES
     frames = o_h.shape[1]
     rows = 16
@@ -112,14 +116,14 @@
 
     def summarize(c, before):
         start = pl.multiple_of(c * CHUNK, CHUNK)
-        decay = d_v[pl.ds(start, CHUNK), :]
-        gap = jnp.zeros((CHUNK, 64 - heads), F32)
-        decay = jnp.concatenate([decay, gap, decay, gap], axis=1)
+        decay = d_v[:, pl.ds(start, CHUNK)]
         high = decay.astype(BF16)
         left = decay - high.astype(F32)
         middle = left.astype(BF16)
         low = (left - middle.astype(F32)).astype(BF16)
-        both = dot(cum_l[...], jnp.concatenate([high, middle, low], axis=0))
+        parts = jnp.concatenate([high, middle, low], axis=1)
+        gap = jnp.zeros((64 - heads, parts.shape[1]), BF16)
+        both = dot_t(cum_l[...], jnp.concatenate([parts, gap, parts, gap], axis=0))
         running, running_p = both[0:CHUNK], both[CHUNK : 2 * CHUNK]
         ref = running[CHUNK // 2 - 1 : CHUNK // 2]
         total = running[CHUNK - 1 : CHUNK]
@@ -128,15 +132,13 @@
         row = iota((16, 128), 0)
         extra = jnp.where(row == 0, ref, jnp.where(row == 1, total, total - ref))
         factors = two_parts(jnp.exp(jnp.concatenate([ref - running, extra], axis=0)))
-        writes = w_v[pl.ds(start, CHUNK), :]
+        writes = w_v[:, pl.ds(start, CHUNK)]
         pltpu.make_async_copy(x_h.at[c], x_v.at[c], x_sem.at[c]).wait()
         for t in range(tiles):
             cols = slice(t * LANES, (t + 1) * LANES)
             full = dot(factors, expand[:, cols])
             scaled = (x_v[c, :, cols].astype(F32) * full[0:CHUNK]).astype(BF16)
-            own = lax.dot_general(
-                writes, scaled, (((0,), (0,)), ((), ())), preferred_element_type=F32
-            )
+            own = dot(writes, scaled)
             earlier = state[:, cols]
             xs_v[c, t, 0:CHUNK] = scaled
             xs_v[c, t, CHUNK : CHUNK + 64] = (earlier * full[CHUNK : CHUNK + 1]).astype(BF16)
@@ -186,12 +188,9 @@
 
     def local(c, _):
         start = pl.multiple_of(c * CHUNK, CHUNK)
-        reads = dot(perm[...], r_v[pl.ds(start, CHUNK), :]).astype(BF16)
+        reads = dot_t(perm[...], r_v[:, pl.ds(start, CHUNK)]).astype(BF16)
         rp_v[pl.ds(start, CHUNK), :] = reads
-        scores = lax.dot_general(
-            reads, w_v[pl.ds(start, CHUNK), :], (((1,), (1,)), ((), ())),
-            preferred_element_type=F32,
-        )
+        scores = dot(reads, w_v[:, pl.ds(start, CHUNK)])
         masked = jnp.where(causal, scores, 0.0).astype(BF16)
         left = jnp.concatenate([masked, reads], axis=1)
         factors = two_parts(jnp.exp(jnp.concatenate([out_arg[c], dev_arg[c]], axis=0)))
@@ -246,7 +245,7 @@
     def norm(t, _):
         first = pl.multiple_of(t * LANES, LANES)
         entering = enter[:, pl.ds(first, LANES)].astype(BF16)
-        gain = g_v[:, pl.ds(first, LANES)]
+        gain = jnp.concatenate([g_v[pl.ds(2 * t, 1), :], g_v[pl.ds(2 * t + 1, 1), :]], axis=1)
         for b in range(chunks // 2):
             part = slice(2 * b * CHUNK, 2 * (b + 1) * CHUNK)
             mixed = ml_v[t, part] + od_v[t, part] * dot(rp_v[part], entering)
@@ -288,20 +287,15 @@
 
     lax.fori_loop(0, tiles, deliver, 0)
 
-    def put(t):
-        return pltpu.make_async_copy(
-            out_v.at[t], out_h.at[:, pl.ds(pl.multiple_of(t * LANES, LANES), LANES)], out_sem
-        )
-
     def arrive(t, _):
         part = recv3.at[t, pl.ds(0, n - 1)]
         pltpu.make_async_copy(part, part, del_r_sem.at[t]).wait()
-        out_v[t] = dot(sel_r[...], recv3[t].reshape(n * rows, LANES)).astype(BF16)
-        put(t).start()
+        out_h[:, pl.ds(pl.multiple_of(t * LANES, LANES), LANES)] = dot(
+            sel_r[...], recv3[t].reshape(n * rows, LANES)
+        ).astype(BF16)
         return 0
 
     lax.fori_loop(0, tiles, arrive, 0)
-    pltpu.make_async_copy(out_v, out_v, out_sem).wait()
     one_meta = meta_r.at[pl.ds(0, n - 1)]
     pltpu.make_async_copy(one_meta, one_meta, meta_sem.at[0]).wait()
     all_of(send1, one_sem.at[0])
@@ -325,18 +319,18 @@
     deep, out_width = merge_weight.shape
     assert (n, state_size, width, out_width, frames) == (32, 64, 1536, 1536, 16)
     vmem, dma = pltpu.VMEM, pltpu.SemaphoreType.DMA
-    anywhere = pl.BlockSpec(memory_space=pl.ANY)
+    in_place = pl.BlockSpec(memory_space=pltpu.HBM)
     return pl.pallas_call(
         functools.partial(kernel, n),
-        out_shape=jax.ShapeDtypeStruct((n * 16, out_width), BF16),
-        in_specs=[anywhere] * 7,
-        out_specs=anywhere,
+        out_shape=pltpu.VMEM((n * 16, out_width), BF16),
+        in_specs=[in_place] * 7,
+        out_specs=pl.BlockSpec(memory_space=pltpu.VMEM),
         scratch_shapes=[
             vmem((chunks, CHUNK, width), BF16),
-            vmem(writer.shape, BF16),
-            vmem(reader.shape, BF16),
-            vmem(log_decay.shape, F32),
-            vmem((1, width), F32),
+            vmem(writer.shape[::-1], BF16),
+            vmem(reader.shape[::-1], BF16),
+            vmem(log_decay.shape[::-1], F32),
+            vmem((width // 128, 128), F32),
             vmem((1, frames), jnp.int32),
             vmem((tiles, deep, LANES), BF16),
             vmem((2 * CHUNK, 3 * CHUNK), BF16),
@@ -363,11 +357,9 @@
             vmem((n * 16, n * 16), BF16),
             vmem((tiles, n, 16, LANES), BF16),
             vmem((tiles, n, 16, LANES), BF16),
-            vmem((tiles, n * 16, LANES), BF16),
             dma((chunks,)),
             dma((5,)),
             dma((tiles,)),
-            dma,
             dma((2,)),
             dma((2,)),
             dma((2,)),
@@ -375,16 +367,21 @@
             dma((tiles,)),
         ],
         compiler_params=pltpu.CompilerParams(
-            collective_id=0, has_side_effects=True, vmem_limit_bytes=62 * 1024 * 1024
+            collective_id=0, has_side_effects=True, vmem_limit_bytes=52 * 1024 * 1024
         ),
     )(
-        heads_in.reshape(chunks, CHUNK, width),
-        writer,
-        reader,
-        log_decay,
-        norm_gain.reshape(1, width),
-        frame_owner.reshape(1, frames),
-        merge_weight,
+        *(
+            pltpu.with_memory_space_constraint(array, pltpu.HBM)
+            for array in (
+                heads_in.reshape(chunks, CHUNK, width),
+                writer.T,
+                reader.T,
+                log_decay.T,
+                norm_gain.reshape(width // 128, 128),
+                frame_owner.reshape(1, frames),
+                merge_weight,
+            )
+        )
     )
 
 

time: 70 us -> 60.3 us (0.86)
  local copies, waits for them, and re-layouts: 9.37 us -> 1.15 us
  Pallas kernels: 60.4 us -> 59.1 us
    unnamed x4 -> x1, local copies, waits for them, and re-layouts: 8.07 us -> 1.15 us
    pallas_call x1, Pallas kernels: 60.4 us -> 59.1 us  [shards(): pl.pallas_call(functools.partial(kernel, n), out_shape=pltpu.VMEM((n * 16...]
    reshape x1 -> x0, local copies, waits for them, and re-layouts: 1.3 us -> none  [shards(): norm_gain.reshape(1, width)]
where the time goes in v2:
time: 60.3 us; the launch traced here: 60.2 us
  Pallas kernels  59.1 us (98%)
  local copies, waits for them, and re-layouts  1.15 us (2%)
    pallas_call x1, Pallas kernels, shards(): pl.pallas_call(functools.partial(kernel, n), out_shape=pltpu.VMEM((n * 16...  59.1 us

profile of v2, /device:TPU:1, one launch (start us, length us, event | category | flops | bytes accessed | tf_op | source)
XLA Modules:
  0.0 60.2 jit_solution(6769798944259225886)
XLA Ops:
  0.0 59.1 %shard_map.73 = bf16[512,1536]{1,0:T(8,128)(2,1)S(1)} custom-call(bf16[8,128,1536]{2,1,0:T(8,128)(2,1)} %bitcast.6, bf16[64,1024]{1,0:T(8,128)(2,1)} %bitcast.8, bf16[64,1024]{1,0:T(8,128)(2,1)} %bitcast.9, f32[48,1024]{1,0:T(8,128)} %bitcast.7, f32[12,128]{1,0:T(8,128)} %bitcast.10, s32[1,16]{1,0:T(1,128)} %bitcast.11, bf16[6144,1536]{1,0:T(8,128)(2,1)} %wm_h.1), custom_call_target="tpu_custom_call" | custom-call | tf_op jit(solution)/shard_map/pallas_call | solution.py:323
  59.1 1.1 %copy.9 = bf16[512,1536]{1,0:T(8,128)(2,1)} copy(bf16[512,1536]{1,0:T(8,128)(2,1)S(1)} %shard_map.73) | data formatting | bytes 3145728

commit v3 on v2

--- a/solution.py
+++ b/solution.py
@@ -48,12 +48,13 @@
 def kernel(
     n, x_h, w_h, r_h, d_h, g_h, o_h, wm_h, out_h,
     x_v, w_v, r_v, d_v, g_v, o_v, wm_v,
-    cum_l, expand, block_diag, perm, xs_v, out_arg, dev_arg, state, rp_v, ml_v, od_v, a_v,
+    cum_l, expand, block_diag, perm, xs_v, in_factor, out_arg, out_factor, left_v, state, rp_v, ml_v, od_v, a_v,
     meta_s, meta_r, send1, recv1, decays, send2, recv2, enter, sel_s, sel_r, send3, recv3,
     x_sem, in_sem, wm_sem, meta_sem, one_sem, two_sem, del_s_sem, del_r_sem,
 ):
     me = lax.axis_index("span")
-    chunks, _, width = x_v.shape
+    tokens, width = x_h.shape
+    chunks = tokens // CHUNK
     heads = d_h.shape[0]
     tiles = width // LANES
     frames = o_h.shape[1]
@@ -63,12 +64,17 @@
         pltpu.make_async_copy(s, d, in_sem.at[k])
         for k, (s, d) in enumerate(((d_h, d_v), (w_h, w_v), (r_h, r_v), (g_h, g_v), (o_h, o_v)))
     ]
-    loads = [pltpu.make_async_copy(x_h.at[c], x_v.at[c], x_sem.at[c]) for c in range(chunks)]
-    weights = [
-        pltpu.make_async_copy(wm_h.at[:, pl.ds(t * LANES, LANES)], wm_v.at[t], wm_sem.at[t])
-        for t in range(tiles)
-    ]
-    for copy in small + loads + weights:
+
+    def columns(t):
+        return pl.ds(pl.multiple_of(t * LANES, LANES), LANES)
+
+    def load(t):
+        return pltpu.make_async_copy(x_h.at[:, columns(t)], x_v.at[t], x_sem.at[t])
+
+    def load_weight(t):
+        return pltpu.make_async_copy(wm_h.at[:, columns(t)], wm_v.at[t], wm_sem.at[t])
+
+    for copy in small + [load(t) for t in range(tiles)]:
         copy.start()
 
     barrier = pltpu.get_barrier_semaphore()
@@ -93,10 +99,9 @@
     expand[...] = ones_where(
         (iota((128, width), 0) & 63) == (iota((128, width), 1) >> head_dim_shift)
     )
-    block_diag[...] = ones_where(
-        (iota((LANES, LANES), 0) >> 6) == (iota((LANES, LANES), 1) >> 6)
-    )
-    state[...] = jnp.zeros_like(state)
+    block_diag[...] = jnp.where(
+        (iota((LANES, LANES), 0) >> 6) == (iota((LANES, LANES), 1) >> 6), 1.0 / GROUP, 0.0
+    ).astype(BF16)
     meta_s[...] = jnp.full(meta_s.shape, -1.0, F32)
     for copy in small:
         copy.wait()
@@ -114,9 +119,10 @@
         & ((iota(shape, 0) & 15) == (iota(shape, 1) & 15))
     )
 
-    def summarize(c, before):
-        start = pl.multiple_of(c * CHUNK, CHUNK)
-        decay = d_v[:, pl.ds(start, CHUNK)]
+    before = jnp.zeros((1, 128), F32)
+    for c in range(chunks):
+        part = slice(c * CHUNK, (c + 1) * CHUNK)
+        decay = d_v[:, part]
         high = decay.astype(BF16)
         left = decay - high.astype(F32)
         middle = left.astype(BF16)
@@ -127,28 +133,30 @@
         running, running_p = both[0:CHUNK], both[CHUNK : 2 * CHUNK]
         ref = running[CHUNK // 2 - 1 : CHUNK // 2]
         total = running[CHUNK - 1 : CHUNK]
-        out_arg[c] = running_p - ref
-        dev_arg[c] = running_p + before
+        out_arg[c, 0:CHUNK] = running_p - ref
+        out_arg[c, CHUNK : 2 * CHUNK] = running_p + before
         row = iota((16, 128), 0)
         extra = jnp.where(row == 0, ref, jnp.where(row == 1, total, total - ref))
-        factors = two_parts(jnp.exp(jnp.concatenate([ref - running, extra], axis=0)))
-        writes = w_v[:, pl.ds(start, CHUNK)]
-        pltpu.make_async_copy(x_h.at[c], x_v.at[c], x_sem.at[c]).wait()
-        for t in range(tiles):
-            cols = slice(t * LANES, (t + 1) * LANES)
-            full = dot(factors, expand[:, cols])
-            scaled = (x_v[c, :, cols].astype(F32) * full[0:CHUNK]).astype(BF16)
-            own = dot(writes, scaled)
-            earlier = state[:, cols]
+        in_factor[c] = two_parts(jnp.exp(jnp.concatenate([ref - running, extra], axis=0)))
+        before = before + total
+    meta_s[0:1, :] = before
+
+    def summarize(t, _):
+        load(t).wait()
+        spread = expand[:, columns(t)]
+        carry = jnp.zeros((w_v.shape[0], LANES), F32)
+        for c in range(chunks):
+            part = slice(c * CHUNK, (c + 1) * CHUNK)
+            full = dot(in_factor[c], spread)
+            scaled = (x_v[t, part].astype(F32) * full[0:CHUNK]).astype(BF16)
+            own = dot(w_v[:, part], scaled)
             xs_v[c, t, 0:CHUNK] = scaled
-            xs_v[c, t, CHUNK : CHUNK + 64] = (earlier * full[CHUNK : CHUNK + 1]).astype(BF16)
-            state[:, cols] = (
-                earlier * full[CHUNK + 1 : CHUNK + 2] + own * full[CHUNK + 2 : CHUNK + 3]
-            )
-        return before + total
-
-    total = lax.fori_loop(0, chunks, summarize, jnp.zeros((1, 128), F32))
-    meta_s[0:1, :] = total
+            xs_v[c, t, CHUNK : CHUNK + 64] = (carry * full[CHUNK : CHUNK + 1]).astype(BF16)
+            carry = carry * full[CHUNK + 1 : CHUNK + 2] + own * full[CHUNK + 2 : CHUNK + 3]
+        state[:, columns(t)] = carry
+        return 0
+
+    lax.fori_loop(0, tiles, summarize, 0)
     for a in range(8):
         for b in range(4):
             send1[a * 4 + b] = state[8 * a : 8 * a + 8, 384 * b : 384 * b + 384].astype(BF16)
@@ -181,33 +189,53 @@
         return 0
 
     lax.fori_loop(1, n, send_one, 0)
+    for t in range(tiles):
+        load_weight(t).start()
     meta_r[me] = meta_s[...]
     recv1[me] = send1[me]
 
     causal = iota((CHUNK, CHUNK), 1) <= token_of_row(iota((CHUNK, CHUNK), 0))
 
-    def local(c, _):
-        start = pl.multiple_of(c * CHUNK, CHUNK)
-        reads = dot_t(perm[...], r_v[:, pl.ds(start, CHUNK)]).astype(BF16)
-        rp_v[pl.ds(start, CHUNK), :] = reads
-        scores = dot(reads, w_v[:, pl.ds(start, CHUNK)])
-        masked = jnp.where(causal, scores, 0.0).astype(BF16)
-        left = jnp.concatenate([masked, reads], axis=1)
-        factors = two_parts(jnp.exp(jnp.concatenate([out_arg[c], dev_arg[c]], axis=0)))
-        for t in range(tiles):
-            full = dot(factors, expand[:, t * LANES : (t + 1) * LANES])
-            mixed = dot(left, xs_v[c, t])
-            ml_v[t, pl.ds(start, CHUNK), :] = mixed * full[0:CHUNK]
-            od_v[t, pl.ds(start, CHUNK), :] = full[CHUNK : 2 * CHUNK]
-        return 0
-
-    lax.fori_loop(0, chunks, local, 0)
+    for c in range(chunks):
+        part = slice(c * CHUNK, (c + 1) * CHUNK)
+        reads = dot_t(perm[...], r_v[:, part]).astype(BF16)
+        scores = dot(reads, w_v[:, part])
+        rp_v[part] = reads
+        left_v[c] = jnp.concatenate([jnp.where(causal, scores, 0.0).astype(BF16), reads], axis=1)
+        out_factor[c] = two_parts(jnp.exp(out_arg[c]))
+
+    def local(t, _):
+        spread = expand[:, columns(t)]
+        for c in range(chunks):
+            part = slice(c * CHUNK, (c + 1) * CHUNK)
+            full = dot(out_factor[c], spread)
+            ml_v[t, part] = dot(left_v[c], xs_v[c, t]) * full[0:CHUNK]
+            od_v[t, part] = full[CHUNK : 2 * CHUNK]
+        return 0
+
+    lax.fori_loop(0, tiles // 2, local, 0)
 
     all_of(meta_r, meta_sem.at[1])
     totals = meta_r[:, 0, :]
     factors = two_parts(jnp.exp(totals))
     for b in range(4):
         decays[b] = dot(factors, expand[:, 384 * b : 384 * b + 384])
+    all_of(recv1, one_sem.at[1])
+    quarter = lax.rem(me, 4)
+    carry = jnp.zeros(recv1.shape[1:], F32)
+    for i in range(n):
+        send2[i] = carry.astype(BF16)
+        if i < n - 1:
+            carry = carry * decays[quarter, i : i + 1, :] + recv1[i].astype(F32)
+
+    def send_two(k, _):
+        d = lax.rem(me + k, n)
+        remote(send2.at[d], recv2.at[me], two_sem, d).start()
+        return 0
+
+    lax.fori_loop(1, n, send_two, 0)
+    recv2[me] = send2[me]
+    lax.fori_loop(tiles // 2, tiles, local, 0)
     owned = jnp.max(jnp.where(meta_r[:, 1, :] == me.astype(F32), 1.0, 0.0), axis=1, keepdims=True)
     owned = jnp.broadcast_to(owned, (n, 128))
     rank = dot(ones_where(iota((n, n), 1) < iota((n, n), 0)), owned.astype(BF16))
@@ -222,35 +250,19 @@
         & ((iota(shape, 0) & 15) == (iota(shape, 1) & 15))
     )
 
-    all_of(recv1, one_sem.at[1])
-    quarter = lax.rem(me, 4)
-    carry = jnp.zeros(recv1.shape[1:], F32)
-    for i in range(n):
-        send2[i] = carry.astype(BF16)
-        if i < n - 1:
-            carry = carry * decays[quarter, i : i + 1, :] + recv1[i].astype(F32)
-
-    def send_two(k, _):
-        d = lax.rem(me + k, n)
-        remote(send2.at[d], recv2.at[me], two_sem, d).start()
-        return 0
-
-    lax.fori_loop(1, n, send_two, 0)
-    recv2[me] = send2[me]
     all_of(recv2, two_sem.at[1])
     for a in range(8):
         for b in range(4):
             enter[8 * a : 8 * a + 8, 384 * b : 384 * b + 384] = recv2[a * 4 + b].astype(F32)
 
     def norm(t, _):
-        first = pl.multiple_of(t * LANES, LANES)
-        entering = enter[:, pl.ds(first, LANES)].astype(BF16)
+        entering = enter[:, columns(t)].astype(BF16)
         gain = jnp.concatenate([g_v[pl.ds(2 * t, 1), :], g_v[pl.ds(2 * t + 1, 1), :]], axis=1)
         for b in range(chunks // 2):
             part = slice(2 * b * CHUNK, 2 * (b + 1) * CHUNK)
             mixed = ml_v[t, part] + od_v[t, part] * dot(rp_v[part], entering)
             squares = dot((mixed * mixed).astype(BF16), block_diag[...])
-            normed = mixed * lax.rsqrt(squares * (1.0 / GROUP) + EPSILON) * gain
+            normed = mixed * lax.rsqrt(squares + EPSILON) * gain
             normed = normed.astype(BF16)
             for c in range(2):
                 for q in range(4):
@@ -263,9 +275,7 @@
     lax.fori_loop(0, tiles, norm, 0)
 
     def deliver(t, _):
-        pltpu.make_async_copy(
-            wm_h.at[:, pl.ds(pl.multiple_of(t * LANES, LANES), LANES)], wm_v.at[t], wm_sem.at[t]
-        ).wait()
+        load_weight(t).wait()
         merged = dot(a_v[...], wm_v[t]).astype(BF16)
         send3[t] = dot(sel_s[...], merged).astype(BF16).reshape(n, rows, LANES)
 
@@ -290,7 +300,7 @@
     def arrive(t, _):
         part = recv3.at[t, pl.ds(0, n - 1)]
         pltpu.make_async_copy(part, part, del_r_sem.at[t]).wait()
-        out_h[:, pl.ds(pl.multiple_of(t * LANES, LANES), LANES)] = dot(
+        out_h[:, columns(t)] = dot(
             sel_r[...], recv3[t].reshape(n * rows, LANES)
         ).astype(BF16)
         return 0
@@ -326,7 +336,7 @@
         in_specs=[in_place] * 7,
         out_specs=pl.BlockSpec(memory_space=pltpu.VMEM),
         scratch_shapes=[
-            vmem((chunks, CHUNK, width), BF16),
+            vmem((tiles, tokens, LANES), BF16),
             vmem(writer.shape[::-1], BF16),
             vmem(reader.shape[::-1], BF16),
             vmem(log_decay.shape[::-1], F32),
@@ -338,8 +348,10 @@
             vmem((LANES, LANES), BF16),
             vmem((CHUNK, CHUNK), BF16),
             vmem((chunks, tiles, CHUNK + state_size, LANES), BF16),
-            vmem((chunks, CHUNK, 128), F32),
-            vmem((chunks, CHUNK, 128), F32),
+            vmem((chunks, CHUNK + 16, 128), BF16),
+            vmem((chunks, 2 * CHUNK, 128), F32),
+            vmem((chunks, 2 * CHUNK, 128), BF16),
+            vmem((chunks, CHUNK, CHUNK + state_size), BF16),
             vmem((state_size, width), F32),
             vmem((tokens, state_size), BF16),
             vmem((tiles, tokens, LANES), F32),
@@ -357,7 +369,7 @@
             vmem((n * 16, n * 16), BF16),
             vmem((tiles, n, 16, LANES), BF16),
             vmem((tiles, n, 16, LANES), BF16),
-            dma((chunks,)),
+            dma((tiles,)),
             dma((5,)),
             dma((tiles,)),
             dma((2,)),
@@ -373,7 +385,7 @@
         *(
             pltpu.with_memory_space_constraint(array, pltpu.HBM)
             for array in (
-                heads_in.reshape(chunks, CHUNK, width),
+                heads_in,
                 writer.T,
                 reader.T,
                 log_decay.T,

time: 60.3 us -> 55.1 us (0.914)
  Pallas kernels: 59.1 us -> 53.8 us
    pallas_call x1, Pallas kernels: 59.1 us -> 53.8 us  [shards(): pl.pallas_call(functools.partial(kernel, n), out_shape=pltpu.VMEM((n * 16...]
where the time goes in v3:
time: 55.1 us; the launch traced here: 55 us
  Pallas kernels  53.8 us (98%)
  local copies, waits for them, and re-layouts  1.15 us (2%)
    pallas_call x1, Pallas kernels, shards(): pl.pallas_call(functools.partial(kernel, n), out_shape=pltpu.VMEM((n * 16...  53.8 us
    unnamed x1, local copies, waits for them, and re-layouts  1.15 us

profile of v3, /device:TPU:1, one launch (start us, length us, event | category | flops | bytes accessed | tf_op | source)
XLA Modules:
  0.0 55.0 jit_solution(7656463194616357643)
XLA Ops:
  0.0 53.8 %shard_map.73 = bf16[512,1536]{1,0:T(8,128)(2,1)S(1)} custom-call(bf16[1024,1536]{1,0:T(8,128)(2,1)} %x_h.1, bf16[64,1024]{1,0:T(8,128)(2,1)} %bitcast.6, bf16[64,1024]{1,0:T(8,128)(2,1)} %bitcast.7, f32[48,1024]{1,0:T(8,128)} %bitcast.5, f32[12,128]{1,0:T(8,128)} %bitcast.8, s32[1,16]{1,0:T(1,128)} %bitcast.9, bf16[6144,1536]{1,0:T(8,128)(2,1)} %wm_h.1), custom_call_target="tpu_custom_call" | custom-call | tf_op jit(solution)/shard_map/pallas_call | solution.py:333
  53.8 1.1 %copy.9 = bf16[512,1536]{1,0:T(8,128)(2,1)} copy(bf16[512,1536]{1,0:T(8,128)(2,1)S(1)} %shard_map.73) | data formatting | bytes 3145728

commit v4 on v3

--- a/solution.py
+++ b/solution.py
@@ -145,14 +145,21 @@
         load(t).wait()
         spread = expand[:, columns(t)]
         carry = jnp.zeros((w_v.shape[0], LANES), F32)
-        for c in range(chunks):
-            part = slice(c * CHUNK, (c + 1) * CHUNK)
-            full = dot(in_factor[c], spread)
-            scaled = (x_v[t, part].astype(F32) * full[0:CHUNK]).astype(BF16)
-            own = dot(w_v[:, part], scaled)
-            xs_v[c, t, 0:CHUNK] = scaled
-            xs_v[c, t, CHUNK : CHUNK + 64] = (carry * full[CHUNK : CHUNK + 1]).astype(BF16)
-            carry = carry * full[CHUNK + 1 : CHUNK + 2] + own * full[CHUNK + 2 : CHUNK + 3]
+        full, scaled = {}, {}
+        for k in range(chunks + 2):
+            if k < chunks:
+                full[k] = dot(in_factor[k], spread)
+            c = k - 1
+            if 0 <= c < chunks:
+                part = slice(c * CHUNK, (c + 1) * CHUNK)
+                scaled[c] = (x_v[t, part].astype(F32) * full[c][0:CHUNK]).astype(BF16)
+                xs_v[c, t, 0:CHUNK] = scaled[c]
+            c = k - 2
+            if c >= 0:
+                own = dot(w_v[:, c * CHUNK : (c + 1) * CHUNK], scaled.pop(c))
+                scales = full.pop(c)[CHUNK : CHUNK + 3]
+                xs_v[c, t, CHUNK : CHUNK + 64] = (carry * scales[0:1]).astype(BF16)
+                carry = carry * scales[1:2] + own * scales[2:3]
         state[:, columns(t)] = carry
         return 0
 
@@ -258,18 +265,21 @@
     def norm(t, _):
         entering = enter[:, columns(t)].astype(BF16)
         gain = jnp.concatenate([g_v[pl.ds(2 * t, 1), :], g_v[pl.ds(2 * t + 1, 1), :]], axis=1)
-        for b in range(chunks // 2):
-            part = slice(2 * b * CHUNK, 2 * (b + 1) * CHUNK)
-            mixed = ml_v[t, part] + od_v[t, part] * dot(rp_v[part], entering)
-            squares = dot((mixed * mixed).astype(BF16), block_diag[...])
-            normed = mixed * lax.rsqrt(squares + EPSILON) * gain
-            normed = normed.astype(BF16)
-            for c in range(2):
+        mixed, squares = {}, {}
+        for k in range(chunks + 2):
+            if k < chunks:
+                part = slice(k * CHUNK, (k + 1) * CHUNK)
+                mixed[k] = ml_v[t, part] + od_v[t, part] * dot(rp_v[part], entering)
+            c = k - 1
+            if 0 <= c < chunks:
+                squares[c] = dot((mixed[c] * mixed[c]).astype(BF16), block_diag[...])
+            c = k - 2
+            if c >= 0:
+                normed = mixed.pop(c) * lax.rsqrt(squares.pop(c) + EPSILON) * gain
+                normed = normed.astype(BF16)
                 for q in range(4):
-                    a_v[
-                        (2 * b + c) * 32 : (2 * b + c + 1) * 32,
-                        pl.ds(pl.multiple_of(q * width + t * LANES, LANES), LANES),
-                    ] = normed[c * CHUNK + q * 32 : c * CHUNK + (q + 1) * 32]
+                    first = pl.multiple_of(q * width + t * LANES, LANES)
+                    a_v[c * 32 : (c + 1) * 32, pl.ds(first, LANES)] = normed[q * 32 : (q + 1) * 32]
         return 0
 
     lax.fori_loop(0, tiles, norm, 0)

time: 55.1 us -> 50 us (0.907)
  Pallas kernels: 53.8 us -> 48.8 us
    pallas_call x1, Pallas kernels: 53.8 us -> 48.8 us  [shards(): pl.pallas_call(functools.partial(kernel, n), out_shape=pltpu.VMEM((n * 16...]
where the time goes in v4:
time: 50 us; the launch traced here: 49.9 us
  Pallas kernels  48.8 us (98%)
  local copies, waits for them, and re-layouts  1.15 us (2%)
    pallas_call x1, Pallas kernels, shards(): pl.pallas_call(functools.partial(kernel, n), out_shape=pltpu.VMEM((n * 16...  48.8 us
    unnamed x1, local copies, waits for them, and re-layouts  1.15 us

profile of v4, /device:TPU:1, one launch (start us, length us, event | category | flops | bytes accessed | tf_op | source)
XLA Modules:
  0.0 49.9 jit_solution(4411706925381478238)
XLA Ops:
  0.0 48.8 %shard_map.73 = bf16[512,1536]{1,0:T(8,128)(2,1)S(1)} custom-call(bf16[1024,1536]{1,0:T(8,128)(2,1)} %x_h.1, bf16[64,1024]{1,0:T(8,128)(2,1)} %bitcast.6, bf16[64,1024]{1,0:T(8,128)(2,1)} %bitcast.7, f32[48,1024]{1,0:T(8,128)} %bitcast.5, f32[12,128]{1,0:T(8,128)} %bitcast.8, s32[1,16]{1,0:T(1,128)} %bitcast.9, bf16[6144,1536]{1,0:T(8,128)(2,1)} %wm_h.1), custom_call_target="tpu_custom_call" | custom-call | tf_op jit(solution)/shard_map/pallas_call | solution.py:343
  48.8 1.1 %copy.9 = bf16[512,1536]{1,0:T(8,128)(2,1)} copy(bf16[512,1536]{1,0:T(8,128)(2,1)S(1)} %shard_map.73) | data formatting | bytes 3145728

commit v5 on v4

--- a/solution.py
+++ b/solution.py
@@ -33,6 +33,11 @@
     return jnp.where(condition, 1.0, 0.0).astype(BF16)
 
 
+def slice_of(p):
+    b = (p & 1) * 2 + ((p >> 1) & 1)
+    return slice(8 * (p >> 2), 8 * (p >> 2) + 8), slice(384 * b, 384 * b + 384)
+
+
 def token_of_row(row):
     q, rest = row >> 5, row & 31
     frame, i2, j2 = rest >> 4, (rest >> 2) & 3, rest & 3
@@ -48,7 +53,7 @@
 def kernel(
     n, x_h, w_h, r_h, d_h, g_h, o_h, wm_h, out_h,
     x_v, w_v, r_v, d_v, g_v, o_v, wm_v,
-    cum_l, expand, block_diag, perm, xs_v, in_factor, out_arg, out_factor, left_v, state, rp_v, ml_v, od_v, a_v,
+    cum_l, expand, block_diag, xs_v, in_factor, out_arg, out_factor, left_v, state, rp_v, ml_v, od_v, a_v,
     meta_s, meta_r, send1, recv1, decays, send2, recv2, enter, sel_s, sel_r, send3, recv3,
     x_sem, in_sem, wm_sem, meta_sem, one_sem, two_sem, del_s_sem, del_r_sem,
 ):
@@ -91,7 +96,6 @@
     token = token_of_row(row_l)
     lower = ones_where(col_l <= row_l)
     lower_p = ones_where(col_l <= token)
-    perm[...] = ones_where(col_l == token)
     for k in range(3):
         cum_l[0:CHUNK, k * CHUNK : (k + 1) * CHUNK] = lower
         cum_l[CHUNK : 2 * CHUNK, k * CHUNK : (k + 1) * CHUNK] = lower_p
@@ -99,25 +103,8 @@
     expand[...] = ones_where(
         (iota((128, width), 0) & 63) == (iota((128, width), 1) >> head_dim_shift)
     )
-    block_diag[...] = jnp.where(
-        (iota((LANES, LANES), 0) >> 6) == (iota((LANES, LANES), 1) >> 6), 1.0 / GROUP, 0.0
-    ).astype(BF16)
-    meta_s[...] = jnp.full(meta_s.shape, -1.0, F32)
     for copy in small:
         copy.wait()
-
-    owners = o_v[...].astype(F32)
-    meta_s[1:2, 0:frames] = owners
-    owner_rows = jnp.broadcast_to(owners, (8, frames)).astype(BF16)
-    spread = ones_where(
-        iota((frames, frames * rows), 0) == (iota((frames, frames * rows), 1) >> 4)
-    )
-    owner_row = dot(owner_rows, spread)[0:1]
-    shape = (n * rows, frames * rows)
-    sel_s[...] = ones_where(
-        ((iota(shape, 0) >> 4).astype(F32) == owner_row)
-        & ((iota(shape, 0) & 15) == (iota(shape, 1) & 15))
-    )
 
     before = jnp.zeros((1, 128), F32)
     for c in range(chunks):
@@ -139,7 +126,11 @@
         extra = jnp.where(row == 0, ref, jnp.where(row == 1, total, total - ref))
         in_factor[c] = two_parts(jnp.exp(jnp.concatenate([ref - running, extra], axis=0)))
         before = before + total
-    meta_s[0:1, :] = before
+    owners = o_v[...].astype(F32)
+    own_row = jnp.concatenate(
+        [jnp.zeros((1, 64), F32), owners, jnp.full((1, 64 - frames), -1.0, F32)], axis=1
+    )
+    meta_s[...] = jnp.where(iota((1, 128), 1) < 64, before, own_row)
 
     def summarize(t, _):
         load(t).wait()
@@ -163,13 +154,6 @@
         state[:, columns(t)] = carry
         return 0
 
-    lax.fori_loop(0, tiles, summarize, 0)
-    for a in range(8):
-        for b in range(4):
-            send1[a * 4 + b] = state[8 * a : 8 * a + 8, 384 * b : 384 * b + 384].astype(BF16)
-
-    pl.semaphore_wait(barrier, n - 1)
-
     def remote(source, target, sems, d):
         return pltpu.make_async_remote_copy(
             src_ref=source,
@@ -188,24 +172,40 @@
         remote(meta_s, meta_r.at[me], meta_sem, lax.rem(me + k, n)).start()
         return 0
 
+    def send_half(half):
+        for p in range(half, n, 2):
+            rows8, cols384 = slice_of(p)
+            send1[p] = state[rows8, cols384].astype(BF16)
+
+        def send_one(k, _):
+            d = 2 * lax.rem(me // 2 + k, n // 2) + half
+
+            @pl.when(d != me)
+            def _():
+                remote(send1.at[d], recv1.at[me], one_sem, d).start()
+
+            return 0
+
+        lax.fori_loop(0, n // 2, send_one, 0)
+
+    lax.fori_loop(0, tiles // 2, summarize, 0)
+    pl.semaphore_wait(barrier, n - 1)
     lax.fori_loop(1, n, send_meta, 0)
-
-    def send_one(k, _):
-        d = lax.rem(me + k, n)
-        remote(send1.at[d], recv1.at[me], one_sem, d).start()
-        return 0
-
-    lax.fori_loop(1, n, send_one, 0)
+    send_half(0)
+    lax.fori_loop(tiles // 2, tiles, summarize, 0)
+    send_half(1)
     for t in range(tiles):
         load_weight(t).start()
     meta_r[me] = meta_s[...]
     recv1[me] = send1[me]
 
-    causal = iota((CHUNK, CHUNK), 1) <= token_of_row(iota((CHUNK, CHUNK), 0))
+    token = token_of_row(iota((CHUNK, CHUNK), 0))
+    causal = iota((CHUNK, CHUNK), 1) <= token
+    permute = ones_where(iota((CHUNK, CHUNK), 1) == token)
 
     for c in range(chunks):
         part = slice(c * CHUNK, (c + 1) * CHUNK)
-        reads = dot_t(perm[...], r_v[:, part]).astype(BF16)
+        reads = dot_t(permute, r_v[:, part]).astype(BF16)
         scores = dot(reads, w_v[:, part])
         rp_v[part] = reads
         left_v[c] = jnp.concatenate([jnp.where(causal, scores, 0.0).astype(BF16), reads], axis=1)
@@ -223,12 +223,13 @@
     lax.fori_loop(0, tiles // 2, local, 0)
 
     all_of(meta_r, meta_sem.at[1])
-    totals = meta_r[:, 0, :]
-    factors = two_parts(jnp.exp(totals))
+    meta = meta_r[:, 0, :]
+    totals = meta[:, 0:64]
+    factors = two_parts(jnp.exp(jnp.concatenate([totals, totals], axis=1)))
     for b in range(4):
         decays[b] = dot(factors, expand[:, 384 * b : 384 * b + 384])
     all_of(recv1, one_sem.at[1])
-    quarter = lax.rem(me, 4)
+    quarter = lax.rem(me, 2) * 2 + lax.rem(me // 2, 2)
     carry = jnp.zeros(recv1.shape[1:], F32)
     for i in range(n):
         send2[i] = carry.astype(BF16)
@@ -243,7 +244,21 @@
     lax.fori_loop(1, n, send_two, 0)
     recv2[me] = send2[me]
     lax.fori_loop(tiles // 2, tiles, local, 0)
-    owned = jnp.max(jnp.where(meta_r[:, 1, :] == me.astype(F32), 1.0, 0.0), axis=1, keepdims=True)
+    block_diag[...] = jnp.where(
+        (iota((LANES, LANES), 0) >> 6) == (iota((LANES, LANES), 1) >> 6), 1.0 / GROUP, 0.0
+    ).astype(BF16)
+    owner_rows = jnp.broadcast_to(owners, (8, frames)).astype(BF16)
+    spread = ones_where(
+        iota((frames, frames * rows), 0) == (iota((frames, frames * rows), 1) >> 4)
+    )
+    owner_row = dot(owner_rows, spread)[0:1]
+    shape = (n * rows, frames * rows)
+    sel_s[...] = ones_where(
+        ((iota(shape, 0) >> 4).astype(F32) == owner_row)
+        & ((iota(shape, 0) & 15) == (iota(shape, 1) & 15))
+    )
+    mine = (meta == me.astype(F32)) & (iota(meta.shape, 1) >= 64)
+    owned = jnp.max(jnp.where(mine, 1.0, 0.0), axis=1, keepdims=True)
     owned = jnp.broadcast_to(owned, (n, 128))
     rank = dot(ones_where(iota((n, n), 1) < iota((n, n), 0)), owned.astype(BF16))
     place = jnp.where(owned > 0.0, rank + 1.0, 0.0)[:, 0:1]
@@ -258,9 +273,9 @@
     )
 
     all_of(recv2, two_sem.at[1])
-    for a in range(8):
-        for b in range(4):
-            enter[8 * a : 8 * a + 8, 384 * b : 384 * b + 384] = recv2[a * 4 + b].astype(F32)
+    for p in range(n):
+        rows8, cols384 = slice_of(p)
+        enter[rows8, cols384] = recv2[p].astype(F32)
 
     def norm(t, _):
         entering = enter[:, columns(t)].astype(BF16)
@@ -284,13 +299,22 @@
 
     lax.fori_loop(0, tiles, norm, 0)
 
+    z, y, core = me // 8, lax.rem(me // 2, 4), lax.rem(me, 2)
+    order = sorted(
+        ((dz, dy, dc) for dz in range(4) for dy in range(4) for dc in range(2) if dz + dy + dc),
+        key=lambda o: -min(o[0], 4 - o[0]) - min(o[1], 4 - o[1]),
+    )
+
+    def place_of(dz, dy, dc):
+        return lax.rem(z + dz, 4) * 8 + lax.rem(y + dy, 4) * 2 + lax.rem(core + dc, 2)
+
     def deliver(t, _):
         load_weight(t).wait()
         merged = dot(a_v[...], wm_v[t]).astype(BF16)
         send3[t] = dot(sel_s[...], merged).astype(BF16).reshape(n, rows, LANES)
 
-        def send(k, _):
-            d = lax.rem(me + k, n)
+        for dz, dy, dc in order:
+            d = place_of(dz, dy, dc)
             pltpu.make_async_remote_copy(
                 src_ref=send3.at[t, d],
                 dst_ref=recv3.at[t, me],
@@ -299,9 +323,6 @@
                 device_id={"span": d},
                 device_id_type=MESH,
             ).start()
-            return 0
-
-        lax.fori_loop(1, n, send, 0)
         recv3[t, me] = send3[t, me]
         return 0
 
@@ -356,7 +377,6 @@
             vmem((2 * CHUNK, 3 * CHUNK), BF16),
             vmem((128, width), BF16),
             vmem((LANES, LANES), BF16),
-            vmem((CHUNK, CHUNK), BF16),
             vmem((chunks, tiles, CHUNK + state_size, LANES), BF16),
             vmem((chunks, CHUNK + 16, 128), BF16),
             vmem((chunks, 2 * CHUNK, 128), F32),
@@ -367,8 +387,8 @@
             vmem((tiles, tokens, LANES), F32),
             vmem((tiles, tokens, LANES), F32),
             vmem((tokens // 4, deep), BF16),
-            vmem((8, 128), F32),
-            vmem((n, 8, 128), F32),
+            vmem((1, 128), F32),
+            vmem((n, 1, 128), F32),
             vmem((n, 8, 384), BF16),
             vmem((n, 8, 384), BF16),
             vmem((4, n, 384), F32),

time: 50 us -> 47.7 us (0.954)
  Pallas kernels: 48.8 us -> 46.5 us
    pallas_call x1, Pallas kernels: 48.8 us -> 46.5 us  [shards(): pl.pallas_call(functools.partial(kernel, n), out_shape=pltpu.VMEM((n * 16...]
where the time goes in v5:
time: 47.7 us; the launch traced here: 47.6 us
  Pallas kernels  46.5 us (97%)
  local copies, waits for them, and re-layouts  1.15 us (2%)
    pallas_call x1, Pallas kernels, shards(): pl.pallas_call(functools.partial(kernel, n), out_shape=pltpu.VMEM((n * 16...  46.5 us
    unnamed x1, local copies, waits for them, and re-layouts  1.15 us

profile of v5, /device:TPU:1, one launch (start us, length us, event | category | flops | bytes accessed | tf_op | source)
XLA Modules:
  0.0 47.6 jit_solution(12787971294726592400)
XLA Ops:
  0.0 46.5 %shard_map.73 = bf16[512,1536]{1,0:T(8,128)(2,1)S(1)} custom-call(bf16[1024,1536]{1,0:T(8,128)(2,1)} %x_h.1, bf16[64,1024]{1,0:T(8,128)(2,1)} %bitcast.6, bf16[64,1024]{1,0:T(8,128)(2,1)} %bitcast.7, f32[48,1024]{1,0:T(8,128)} %bitcast.5, f32[12,128]{1,0:T(8,128)} %bitcast.8, s32[1,16]{1,0:T(1,128)} %bitcast.9, bf16[6144,1536]{1,0:T(8,128)(2,1)} %wm_h.1), custom_call_target="tpu_custom_call" | custom-call | tf_op jit(solution)/shard_map/pallas_call | solution.py:364
  46.5 1.1 %copy.9 = bf16[512,1536]{1,0:T(8,128)(2,1)} copy(bf16[512,1536]{1,0:T(8,128)(2,1)S(1)} %shard_map.73) | data formatting | bytes 3145728

commit v6 on v5

--- a/solution.py
+++ b/solution.py
@@ -168,6 +168,15 @@
         part = ref.at[pl.ds(0, n - 1)]
         pltpu.make_async_copy(part, part, sem).wait()
 
+    z, y, core = me // 8, lax.rem(me // 2, 4), lax.rem(me, 2)
+    order = sorted(
+        ((dz, dy, dc) for dz in range(4) for dy in range(4) for dc in range(2) if dz + dy + dc),
+        key=lambda o: -min(o[0], 4 - o[0]) - min(o[1], 4 - o[1]),
+    )
+
+    def place_of(dz, dy, dc):
+        return lax.rem(z + dz, 4) * 8 + lax.rem(y + dy, 4) * 2 + lax.rem(core + dc, 2)
+
     def send_meta(k, _):
         remote(meta_s, meta_r.at[me], meta_sem, lax.rem(me + k, n)).start()
         return 0
@@ -177,16 +186,13 @@
             rows8, cols384 = slice_of(p)
             send1[p] = state[rows8, cols384].astype(BF16)
 
-        def send_one(k, _):
-            d = 2 * lax.rem(me // 2 + k, n // 2) + half
-
-            @pl.when(d != me)
-            def _():
-                remote(send1.at[d], recv1.at[me], one_sem, d).start()
-
-            return 0
-
-        lax.fori_loop(0, n // 2, send_one, 0)
+        for dz, dy, dc in order + [(0, 0, 0)]:
+            if dc == 0:
+                d = lax.rem(z + dz, 4) * 8 + lax.rem(y + dy, 4) * 2 + half
+
+                @pl.when(d != me)
+                def _():
+                    remote(send1.at[d], recv1.at[me], one_sem, d).start()
 
     lax.fori_loop(0, tiles // 2, summarize, 0)
     pl.semaphore_wait(barrier, n - 1)
@@ -236,12 +242,9 @@
         if i < n - 1:
             carry = carry * decays[quarter, i : i + 1, :] + recv1[i].astype(F32)
 
-    def send_two(k, _):
-        d = lax.rem(me + k, n)
+    for dz, dy, dc in order:
+        d = place_of(dz, dy, dc)
         remote(send2.at[d], recv2.at[me], two_sem, d).start()
-        return 0
-
-    lax.fori_loop(1, n, send_two, 0)
     recv2[me] = send2[me]
     lax.fori_loop(tiles // 2, tiles, local, 0)
     block_diag[...] = jnp.where(
@@ -298,15 +301,6 @@
         return 0
 
     lax.fori_loop(0, tiles, norm, 0)
-
-    z, y, core = me // 8, lax.rem(me // 2, 4), lax.rem(me, 2)
-    order = sorted(
-        ((dz, dy, dc) for dz in range(4) for dy in range(4) for dc in range(2) if dz + dy + dc),
-        key=lambda o: -min(o[0], 4 - o[0]) - min(o[1], 4 - o[1]),
-    )
-
-    def place_of(dz, dy, dc):
-        return lax.rem(z + dz, 4) * 8 + lax.rem(y + dy, 4) * 2 + lax.rem(core + dc, 2)
 
     def deliver(t, _):
         load_weight(t).wait()

time: 47.7 us -> 46.7 us (0.979)
  Pallas kernels: 46.5 us -> 45.4 us
    pallas_call x1, Pallas kernels: 46.5 us -> 45.4 us  [shards(): pl.pallas_call(functools.partial(kernel, n), out_shape=pltpu.VMEM((n * 16...]
where the time goes in v6:
time: 46.7 us; the launch traced here: 46.6 us
  Pallas kernels  45.4 us (97%)
  local copies, waits for them, and re-layouts  1.15 us (2%)
    pallas_call x1, Pallas kernels, shards(): pl.pallas_call(functools.partial(kernel, n), out_shape=pltpu.VMEM((n * 16...  45.4 us
    unnamed x1, local copies, waits for them, and re-layouts  1.15 us

profile of v6, /device:TPU:1, one launch (start us, length us, event | category | flops | bytes accessed | tf_op | source)
XLA Modules:
  0.0 46.6 jit_solution(7992488309278739032)
XLA Ops:
  0.0 45.4 %shard_map.73 = bf16[512,1536]{1,0:T(8,128)(2,1)S(1)} custom-call(bf16[1024,1536]{1,0:T(8,128)(2,1)} %x_h.1, bf16[64,1024]{1,0:T(8,128)(2,1)} %bitcast.6, bf16[64,1024]{1,0:T(8,128)(2,1)} %bitcast.7, f32[48,1024]{1,0:T(8,128)} %bitcast.5, f32[12,128]{1,0:T(8,128)} %bitcast.8, s32[1,16]{1,0:T(1,128)} %bitcast.9, bf16[6144,1536]{1,0:T(8,128)(2,1)} %wm_h.1), custom_call_target="tpu_custom_call" | custom-call | tf_op jit(solution)/shard_map/pallas_call | solution.py:358
  45.4 1.1 %copy.9 = bf16[512,1536]{1,0:T(8,128)(2,1)} copy(bf16[512,1536]{1,0:T(8,128)(2,1)S(1)} %shard_map.73) | data formatting | bytes 3145728

commit v7 on v6

--- a/solution.py
+++ b/solution.py
@@ -42,6 +42,12 @@
     q, rest = row >> 5, row & 31
     frame, i2, j2 = rest >> 4, (rest >> 2) & 3, rest & 3
     return frame * 64 + (2 * i2 + (q >> 1)) * 8 + 2 * j2 + (q & 1)
+
+
+def widen(factor, tile):
+    lane = tile * 8 + (iota(factor.shape, 1) >> 5)
+    pick = functools.partial(jnp.take_along_axis, factor, axis=1, mode="promise_in_bounds")
+    return jnp.concatenate([pick(lane), pick(lane + 4)], axis=1)
 
 
 def two_parts(values):
@@ -124,7 +130,7 @@
         out_arg[c, CHUNK : 2 * CHUNK] = running_p + before
         row = iota((16, 128), 0)
         extra = jnp.where(row == 0, ref, jnp.where(row == 1, total, total - ref))
-        in_factor[c] = two_parts(jnp.exp(jnp.concatenate([ref - running, extra], axis=0)))
+        in_factor[c] = jnp.exp(jnp.concatenate([ref - running, extra], axis=0))
         before = before + total
     owners = o_v[...].astype(F32)
     own_row = jnp.concatenate(
@@ -134,12 +140,11 @@
 
     def summarize(t, _):
         load(t).wait()
-        spread = expand[:, columns(t)]
         carry = jnp.zeros((w_v.shape[0], LANES), F32)
         full, scaled = {}, {}
         for k in range(chunks + 2):
             if k < chunks:
-                full[k] = dot(in_factor[k], spread)
+                full[k] = widen(in_factor[k], t)
             c = k - 1
             if 0 <= c < chunks:
                 part = slice(c * CHUNK, (c + 1) * CHUNK)
@@ -372,7 +377,7 @@
             vmem((128, width), BF16),
             vmem((LANES, LANES), BF16),
             vmem((chunks, tiles, CHUNK + state_size, LANES), BF16),
-            vmem((chunks, CHUNK + 16, 128), BF16),
+            vmem((chunks, CHUNK + 16, 128), F32),
             vmem((chunks, 2 * CHUNK, 128), F32),
             vmem((chunks, 2 * CHUNK, 128), BF16),
             vmem((chunks, CHUNK, CHUNK + state_size), BF16),
@@ -403,7 +408,7 @@
             dma((tiles,)),
         ],
         compiler_params=pltpu.CompilerParams(
-            collective_id=0, has_side_effects=True, vmem_limit_bytes=52 * 1024 * 1024
+            collective_id=0, has_side_effects=True, vmem_limit_bytes=54 * 1024 * 1024
         ),
     )(
         *(

time: 46.7 us -> 46.2 us (0.989)
  Pallas kernels: 45.4 us -> 44.9 us
    pallas_call x1, Pallas kernels: 45.4 us -> 44.9 us  [shards(): pl.pallas_call(functools.partial(kernel, n), out_shape=pltpu.VMEM((n * 16...]
where the time goes in v7:
time: 46.2 us; the launch traced here: 46 us
  Pallas kernels  44.9 us (97%)
  local copies, waits for them, and re-layouts  1.15 us (2%)
    pallas_call x1, Pallas kernels, shards(): pl.pallas_call(functools.partial(kernel, n), out_shape=pltpu.VMEM((n * 16...  44.9 us
    unnamed x1, local copies, waits for them, and re-layouts  1.15 us

profile of v7, /device:TPU:1, one launch (start us, length us, event | category | flops | bytes accessed | tf_op | source)
XLA Modules:
  0.0 46.0 jit_solution(15360854051068217140)
XLA Ops:
  0.0 44.9 %shard_map.73 = bf16[512,1536]{1,0:T(8,128)(2,1)S(1)} custom-call(bf16[1024,1536]{1,0:T(8,128)(2,1)} %x_h.1, bf16[64,1024]{1,0:T(8,128)(2,1)} %bitcast.6, bf16[64,1024]{1,0:T(8,128)(2,1)} %bitcast.7, f32[48,1024]{1,0:T(8,128)} %bitcast.5, f32[12,128]{1,0:T(8,128)} %bitcast.8, s32[1,16]{1,0:T(1,128)} %bitcast.9, bf16[6144,1536]{1,0:T(8,128)(2,1)} %wm_h.1), custom_call_target="tpu_custom_call" | custom-call | tf_op jit(solution)/shard_map/pallas_call | solution.py:363
  44.9 1.1 %copy.9 = bf16[512,1536]{1,0:T(8,128)(2,1)} copy(bf16[512,1536]{1,0:T(8,128)(2,1)S(1)} %shard_map.73) | data formatting | bytes 3145728

commit v8 on v7

--- a/solution.py
+++ b/solution.py
@@ -199,11 +199,11 @@
                 def _():
                     remote(send1.at[d], recv1.at[me], one_sem, d).start()
 
-    lax.fori_loop(0, tiles // 2, summarize, 0)
+    lax.fori_loop(0, tiles // 2, summarize, 0, unroll=3)
     pl.semaphore_wait(barrier, n - 1)
     lax.fori_loop(1, n, send_meta, 0)
     send_half(0)
-    lax.fori_loop(tiles // 2, tiles, summarize, 0)
+    lax.fori_loop(tiles // 2, tiles, summarize, 0, unroll=3)
     send_half(1)
     for t in range(tiles):
         load_weight(t).start()
@@ -305,7 +305,7 @@
                     a_v[c * 32 : (c + 1) * 32, pl.ds(first, LANES)] = normed[q * 32 : (q + 1) * 32]
         return 0
 
-    lax.fori_loop(0, tiles, norm, 0)
+    lax.fori_loop(0, tiles, norm, 0, unroll=3)
 
     def deliver(t, _):
         load_weight(t).wait()

time: 46.2 us -> 45.6 us (0.987)
  Pallas kernels: 44.9 us -> 44.3 us
    pallas_call x1, Pallas kernels: 44.9 us -> 44.3 us  [shards(): pl.pallas_call(functools.partial(kernel, n), out_shape=pltpu.VMEM((n * 16...]
where the time goes in v8:
time: 45.6 us; the launch traced here: 45.5 us
  Pallas kernels  44.3 us (97%)
  local copies, waits for them, and re-layouts  1.15 us (3%)
    pallas_call x1, Pallas kernels, shards(): pl.pallas_call(functools.partial(kernel, n), out_shape=pltpu.VMEM((n * 16...  44.3 us
    unnamed x1, local copies, waits for them, and re-layouts  1.15 us

profile of v8, /device:TPU:1, one launch (start us, length us, event | category | flops | bytes accessed | tf_op | source)
XLA Modules:
  0.0 45.5 jit_solution(2154645244014181463)
XLA Ops:
  0.0 44.3 %shard_map.73 = bf16[512,1536]{1,0:T(8,128)(2,1)S(1)} custom-call(bf16[1024,1536]{1,0:T(8,128)(2,1)} %x_h.1, bf16[64,1024]{1,0:T(8,128)(2,1)} %bitcast.6, bf16[64,1024]{1,0:T(8,128)(2,1)} %bitcast.7, f32[48,1024]{1,0:T(8,128)} %bitcast.5, f32[12,128]{1,0:T(8,128)} %bitcast.8, s32[1,16]{1,0:T(1,128)} %bitcast.9, bf16[6144,1536]{1,0:T(8,128)(2,1)} %wm_h.1), custom_call_target="tpu_custom_call" | custom-call | tf_op jit(solution)/shard_map/pallas_call | solution.py:363
  44.3 1.1 %copy.9 = bf16[512,1536]{1,0:T(8,128)(2,1)} copy(bf16[512,1536]{1,0:T(8,128)(2,1)S(1)} %shard_map.73) | data formatting | bytes 3145728

commit v9 on v8

--- a/solution.py
+++ b/solution.py
@@ -305,7 +305,7 @@
                     a_v[c * 32 : (c + 1) * 32, pl.ds(first, LANES)] = normed[q * 32 : (q + 1) * 32]
         return 0
 
-    lax.fori_loop(0, tiles, norm, 0, unroll=3)
+    lax.fori_loop(0, tiles, norm, 0, unroll=6)
 
     def deliver(t, _):
         load_weight(t).wait()

time: 45.6 us -> 45 us (0.987)
  Pallas kernels: 44.3 us -> 43.7 us
    pallas_call x1, Pallas kernels: 44.3 us -> 43.7 us  [shards(): pl.pallas_call(functools.partial(kernel, n), out_shape=pltpu.VMEM((n * 16...]
where the time goes in v9:
time: 45 us; the launch traced here: 44.9 us
  Pallas kernels  43.7 us (97%)
  local copies, waits for them, and re-layouts  1.15 us (3%)
    pallas_call x1, Pallas kernels, shards(): pl.pallas_call(functools.partial(kernel, n), out_shape=pltpu.VMEM((n * 16...  43.7 us
    unnamed x1, local copies, waits for them, and re-layouts  1.15 us

profile of v9, /device:TPU:1, one launch (start us, length us, event | category | flops | bytes accessed | tf_op | source)
XLA Modules:
  0.0 44.9 jit_solution(12712980920278180160)
XLA Ops:
  0.0 43.7 %shard_map.73 = bf16[512,1536]{1,0:T(8,128)(2,1)S(1)} custom-call(bf16[1024,1536]{1,0:T(8,128)(2,1)} %x_h.1, bf16[64,1024]{1,0:T(8,128)(2,1)} %bitcast.6, bf16[64,1024]{1,0:T(8,128)(2,1)} %bitcast.7, f32[48,1024]{1,0:T(8,128)} %bitcast.5, f32[12,128]{1,0:T(8,128)} %bitcast.8, s32[1,16]{1,0:T(1,128)} %bitcast.9, bf16[6144,1536]{1,0:T(8,128)(2,1)} %wm_h.1), custom_call_target="tpu_custom_call" | custom-call | tf_op jit(solution)/shard_map/pallas_call | solution.py:363
  43.7 1.1 %copy.9 = bf16[512,1536]{1,0:T(8,128)(2,1)} copy(bf16[512,1536]{1,0:T(8,128)(2,1)S(1)} %shard_map.73) | data formatting | bytes 3145728
